TPU v7x, 32 devices: a whole 2x2x4 slice. The times are simulated.
32 devices in a mesh: groups: 2 (over y), expert: 4 (over z), section: 4 (over x, core).
Axes of the slice: x: 2, y: 2, z: 4, core: 2. Of those that a mesh axis runs over, the one named last changes fastest.
Arguments:
- pending_microgroups: bfloat16 [4, 1024, 768], P('section', ('groups', 'expert')), parts along dimension 1, may hold values from -6 to 6
- arriving_microgroups: bfloat16 [2, 1024, 768], P(None, ('groups', 'expert')), parts along dimension 1, may hold values from -6 to 6
- expert_choice_grid: int32 [3, 4, 1024], P(None, 'section', ('groups', 'expert')), parts along dimension 2, may hold values from 0 to 1, as said below
- rootmean_gain: float32 [4, 768], P('section'), may hold values from 0.5 to 1.5
- gating_columns: bfloat16 [4, 768, 2], P('section'), may hold values from -0.21875 to 0.21875
- up_projection_matrix: bfloat16 [4, 4, 768, 768], P('section', 'expert'), may hold values from -0.21875 to 0.21875
- down_projection_matrix: bfloat16 [4, 4, 768, 768], P('section', 'expert'), may hold values from -0.21875 to 0.21875
Outputs:
- section_out: bfloat16 [4, 3, 1024, 768], P('section', None, ('groups', 'expert')), parts along dimension 2
There are 2 independent parts, one for each index of `groups`. A program takes and returns all parts, laid end to end along the dimension named above; an argument that names none is the same for every part. Nothing has to cross between parts.
Inputs may be any that keep to these rules, and one draw needn't show every extreme that they name: `expert_choice_grid`: for every tick and section, no expert is named by more than 128 tokens of one aligned block of 128 tokens (the tokens of one device), and one expert, drawn from the seed, is named by exactly 128 tokens of every such block.
All inputs are finite; a program needn't handle non-finite values.
Results may differ from a plain program's by a relative error of at most 0.0095.
Values may be sent and summed in bfloat16 or wider, within the bound.
No kernel may reach another device: no remote copies, remote signals or barrier semaphores. Data moves between devices by JAX's collectives and lax.ppermute only.
A program may use at most 64 MiB of HBM per device.

v0:
```python
import jax
import jax.numpy as jnp
from jax import lax
from jax.sharding import PartitionSpec as P

TICKS = 3


def swapped(x, axis, bit):
    return lax.ppermute(x, axis, [(i, i ^ 1 << bit) for i in range(lax.axis_size(axis))])


def from_behind(value, axis, steps):
    count = lax.axis_size(axis)
    initial, last = (max(0, -steps), min(count, count - steps))
    return lax.ppermute(value, axis, [(source, source + steps) for source in range(initial, last)])


def half_output(received, up_projection_matrix, down_projection_matrix):
    hidden = jnp.maximum(
        jnp.einsum(
            "sid,dh->sih", received, up_projection_matrix, preferred_element_type=jnp.float32
        ),
        0.0,
    ).astype(jnp.bfloat16)
    return jnp.einsum(
        "sih,hd->sid", hidden, down_projection_matrix, preferred_element_type=jnp.float32
    ).astype(jnp.bfloat16)


def expert_layer(
    tok_rows,
    routes,
    rootmean_gain,
    gating_columns,
    up_projection_matrix,
    down_projection_matrix,
    other_in,
    other_out,
):
    num_rows, width = tok_rows.shape
    experts = gating_columns.shape[1]
    capacity = min(num_rows, 3 * num_rows // experts)
    float_rows = tok_rows.astype(jnp.float32)
    inv_rms = lax.rsqrt(jnp.mean(float_rows * float_rows, axis=-1, keepdims=True) + 1e-06)
    normed = (float_rows * inv_rms * rootmean_gain).astype(jnp.bfloat16)
    logits = jnp.dot(normed, gating_columns, preferred_element_type=jnp.float32)
    one_hot = routes[:, None] == jnp.arange(experts, dtype=jnp.int32)[None, :]
    gate_value = jax.nn.sigmoid(jnp.sum(jnp.where(one_hot, logits, 0.0), axis=1))
    flags = one_hot.astype(jnp.int32)
    slot_rank = jnp.sum((jnp.cumsum(flags, axis=0) - flags) * flags, axis=1)
    slot_index = routes * capacity + slot_rank
    placing = (
        slot_index[None, :] == jnp.arange(experts * capacity, dtype=jnp.int32)[:, None]
    ).astype(jnp.bfloat16)
    outgoing = jnp.dot(placing, normed, preferred_element_type=jnp.float32).astype(jnp.bfloat16)
    outgoing = outgoing.reshape(experts, capacity, width)
    halves = outgoing.reshape(2 * experts, capacity // 2, width)
    received = lax.all_to_all(halves, "expert", split_axis=0, concat_axis=0, tiled=True)
    own_part = half_output(received, up_projection_matrix, down_projection_matrix)
    other_part = half_output(received, other_in, other_out)
    summed = (own_part.astype(jnp.float32) + other_part.astype(jnp.float32)).astype(jnp.bfloat16)
    combined = lax.all_to_all(summed, "expert", split_axis=0, concat_axis=0, tiled=True)
    flat_out = combined.reshape(experts * capacity, width)
    expert_out = lax.dot_general(
        placing, flat_out, (((0,), (0,)), ((), ())), preferred_element_type=jnp.float32
    )
    return (float_rows + gate_value[:, None] * expert_out).astype(jnp.bfloat16)


def per_device(
    pending_microgroups,
    arriving_microgroups,
    expert_choice_grid,
    rootmean_gain,
    gating_columns,
    up_projection_matrix,
    down_projection_matrix,
):
    leg_position = lax.axis_index("section")
    own_in = up_projection_matrix[0, 0]
    own_out = down_projection_matrix[0, 0]
    other_in, other_out = swapped((own_in, own_out), "expert", 0)
    running_activation = pending_microgroups[0]
    per_tick = []
    for tick_idx in range(TICKS):
        layer_out = expert_layer(
            running_activation,
            expert_choice_grid[tick_idx, 0],
            rootmean_gain[0],
            gating_columns[0],
            own_in,
            own_out,
            other_in,
            other_out,
        )
        per_tick.append(layer_out)
        if tick_idx + 1 < TICKS:
            moved = from_behind(layer_out, "section", 1)
            running_activation = jnp.where(leg_position == 0, arriving_microgroups[tick_idx], moved)
    return jnp.stack(per_tick)[None]


def solution(mesh):
    placed = (
        P("section", ("groups", "expert"), None),
        P(None, ("groups", "expert"), None),
        P(None, "section", ("groups", "expert")),
        P("section", None),
        P("section", None, None),
        P("section", "expert", None, None),
        P("section", "expert", None, None),
    )
    return jax.shard_map(
        per_device,
        mesh=mesh,
        in_specs=placed,
        out_specs=P("section", None, ("groups", "expert"), None),
        check_vma=False,
    )
```

profile of v0, /device:TPU:0, one launch (start us, length us, event | category | flops | bytes accessed | tf_op | source)
XLA Modules:
  0.0 162.1 jit_solution(12954979192620634909)
XLA Ops:
  0.0 3.1 %collective-permute-start.1 = (bf16[768,768]{1,0:T(8,128)(2,1)}, bf16[768,768]{1,0:T(8,128)(2,1)}, u32[]{:S(2)}, u32[]{:S(2)}) collective-permute-start(bf16[768,768]{1,0:T(8,128)(2,1)} %bitcast.110), channel_id=1, source_target_pairs={{0,4},{4,0},{8,12},{12,8},{1,5},{5,1},{9,13},{13,9},{2,6},{6,2},{1... | collective-permute-start | bytes 3538952 | tf_op jit(solution)/shard_map/ppermute | solution.py:10
  3.1 1.2 fusion.48
  6.9 0.7 reduce
  7.6 1.3 convolution_convert_fusion.8
  8.9 53.5 %all_to_all.30 = bf16[4,64,768]{2,1,0:T(8,128)(2,1)S(1)} all-to-all(bf16[4,64,768]{2,1,0:T(8,128)(2,1)S(1)} %bitcast.105), channel_id=1, replica_groups=mesh['groups'=2,'expert'=4,'section'=4] {'expert'}, dimensions={0} | all-to-all | bytes 786432 | tf_op jit(solution)/shard_map/all_to_all | solution.py:59
  62.3 1.8 %fusion.17 = f32[4,64,768]{2,1,0:T(8,128)} fusion(bf16[4,64,768]{2,1,0:T(8,128)(2,1)S(1)} %all_to_all.30, bf16[1,1,768,768]{3,2,1,0:T(8,128)(2,1)S(1)} %copy-done.3, bf16[1,1,768,768]{3,2,1,0:T(8,128)(2,1)S(1)} %copy-done.4), kind=kOutput, calls=%fused_computation.31 | convolution fusion | flops 604766208 | bytes 3538944 | tf_op jit(solution)/shard_map/sih,hd->sid/dot_general | solution.py:26
  64.1 3.5 %fusion.16 = bf16[4,64,768]{2,1,0:T(8,128)(2,1)} fusion(f32[4,64,768]{2,1,0:T(8,128)} %fusion.17, bf16[4,64,768]{2,1,0:T(8,128)(2,1)S(1)} %all_to_all.30, bf16[768,768]{1,0:T(8,128)(2,1)} %collective-permute-done.1, bf16[768,768]{1,0:T(8,128)(2,1)} %collective-permute-done), kind=kOutput, calls=%fused_computation.29 | convolution fusion | flops 605159424 | bytes 3932160 | tf_op jit(solution)/shard_map/sih,hd->sid/dot_general | solution.py:26
  67.7 3.7 %all-to-all-start.1 = ((bf16[4,64,768]{2,1,0:T(8,128)(2,1)}), bf16[4,64,768]{2,1,0:T(8,128)(2,1)S(1)}, u32[]{:S(2)}, u32[]{:S(2)}) async-start(bf16[4,64,768]{2,1,0:T(8,128)(2,1)} %fusion.16), calls=%async_computation.1 | async-start | bytes 786432 | tf_op jit(solution)/shard_map/all_to_all | solution.py:63
  71.7 10.3 %all-to-all-done.1 = bf16[4,64,768]{2,1,0:T(8,128)(2,1)S(1)} async-done(((bf16[4,64,768]{2,1,0:T(8,128)(2,1)}), bf16[4,64,768]{2,1,0:T(8,128)(2,1)S(1)}, u32[]{:S(2)}, u32[]{:S(2)}) %all-to-all-start.1) | async-done | bytes 393248 | tf_op jit(solution)/shard_map/all_to_all | solution.py:63
  82.2 1.3 collective-permute-start.2
  83.5 1.0 collective-permute-done.2
  85.1 13.0 %all_to_all.31 = bf16[4,64,768]{2,1,0:T(8,128)(2,1)S(1)} all-to-all(bf16[4,64,768]{2,1,0:T(8,128)(2,1)S(1)} %bitcast.106), channel_id=1, replica_groups=mesh['groups'=2,'expert'=4,'section'=4] {'expert'}, dimensions={0} | all-to-all | bytes 786432 | tf_op jit(solution)/shard_map/all_to_all | solution.py:59
  98.0 2.2 %fusion.13 = f32[4,64,768]{2,1,0:T(8,128)S(1)} fusion(bf16[4,64,768]{2,1,0:T(8,128)(2,1)S(1)} %all_to_all.31, bf16[1,1,768,768]{3,2,1,0:T(8,128)(2,1)S(1)} %copy-done.3, bf16[1,1,768,768]{3,2,1,0:T(8,128)(2,1)} %param.12), kind=kOutput, calls=%fused_computation.24 | convolution fusion | flops 604766208 | bytes 3538944 | tf_op jit(solution)/shard_map/sih,hd->sid/dot_general | solution.py:26
  100.2 3.3 %fusion.12 = bf16[4,64,768]{2,1,0:T(8,128)(2,1)} fusion(f32[4,64,768]{2,1,0:T(8,128)S(1)} %fusion.13, bf16[4,64,768]{2,1,0:T(8,128)(2,1)S(1)} %all_to_all.31, bf16[768,768]{1,0:T(8,128)(2,1)} %collective-permute-done.1, bf16[768,768]{1,0:T(8,128)(2,1)} %collective-permute-done), kind=kOutput, calls=%fused_computation.22 | convolution fusion | flops 605159424 | bytes 3932160 | tf_op jit(solution)/shard_map/sih,hd->sid/dot_general | solution.py:26
  103.5 4.3 %all-to-all-start.3 = ((bf16[4,64,768]{2,1,0:T(8,128)(2,1)}), bf16[4,64,768]{2,1,0:T(8,128)(2,1)S(1)}, u32[]{:S(2)}, u32[]{:S(2)}) async-start(bf16[4,64,768]{2,1,0:T(8,128)(2,1)} %fusion.12), calls=%async_computation.3 | async-start | bytes 786432 | tf_op jit(solution)/shard_map/all_to_all | solution.py:63
  108.1 12.2 %all-to-all-done.3 = bf16[4,64,768]{2,1,0:T(8,128)(2,1)S(1)} async-done(((bf16[4,64,768]{2,1,0:T(8,128)(2,1)}), bf16[4,64,768]{2,1,0:T(8,128)(2,1)S(1)}, u32[]{:S(2)}, u32[]{:S(2)}) %all-to-all-start.3) | async-done | bytes 393248 | tf_op jit(solution)/shard_map/all_to_all | solution.py:63
  120.6 2.3 %collective-permute-start.3 = (bf16[128,768]{1,0:T(8,128)(2,1)S(1)}, bf16[128,768]{1,0:T(8,128)(2,1)S(1)}, u32[]{:S(2)}, u32[]{:S(2)}) collective-permute-start(bf16[128,768]{1,0:T(8,128)(2,1)S(1)} %fusion.40), channel_id=1, source_target_pairs={{0,1},{1,2},{2,3},{4,5},{5,6},{6,7},{8,9},{9,10},{10,11},{12,13},{... | collective-permute-start | bytes 589832 | tf_op jit(solution)/shard_map/ppermute | solution.py:16
  123.0 1.0 collective-permute-done.3
  124.5 15.2 %all_to_all.32 = bf16[4,64,768]{2,1,0:T(8,128)(2,1)S(1)} all-to-all(bf16[4,64,768]{2,1,0:T(8,128)(2,1)S(1)} %bitcast.107), channel_id=1, replica_groups=mesh['groups'=2,'expert'=4,'section'=4] {'expert'}, dimensions={0} | all-to-all | bytes 786432 | tf_op jit(solution)/shard_map/all_to_all | solution.py:59
  139.7 2.2 %fusion.9 = f32[4,64,768]{2,1,0:T(8,128)S(1)} fusion(bf16[4,64,768]{2,1,0:T(8,128)(2,1)S(1)} %all_to_all.32, bf16[1,1,768,768]{3,2,1,0:T(8,128)(2,1)S(1)} %copy-done.3, bf16[1,1,768,768]{3,2,1,0:T(8,128)(2,1)} %param.12), kind=kOutput, calls=%fused_computation.17 | convolution fusion | flops 604766208 | bytes 3538944 | tf_op jit(solution)/shard_map/sih,hd->sid/dot_general | solution.py:26
  141.9 3.3 %fusion.8 = bf16[4,64,768]{2,1,0:T(8,128)(2,1)} fusion(f32[4,64,768]{2,1,0:T(8,128)S(1)} %fusion.9, bf16[4,64,768]{2,1,0:T(8,128)(2,1)S(1)} %all_to_all.32, bf16[768,768]{1,0:T(8,128)(2,1)} %collective-permute-done.1, bf16[768,768]{1,0:T(8,128)(2,1)} %collective-permute-done), kind=kOutput, calls=%fused_computation.15 | convolution fusion | flops 605159424 | bytes 3932160 | tf_op jit(solution)/shard_map/sih,hd->sid/dot_general | solution.py:26
  145.2 3.5 %all-to-all-start.5 = ((bf16[4,64,768]{2,1,0:T(8,128)(2,1)}), bf16[4,64,768]{2,1,0:T(8,128)(2,1)S(1)}, u32[]{:S(2)}, u32[]{:S(2)}) async-start(bf16[4,64,768]{2,1,0:T(8,128)(2,1)} %fusion.8), calls=%async_computation.5 | async-start | bytes 786432 | tf_op jit(solution)/shard_map/all_to_all | solution.py:63
  148.9 12.1 %all-to-all-done.5 = bf16[4,64,768]{2,1,0:T(8,128)(2,1)S(1)} async-done(((bf16[4,64,768]{2,1,0:T(8,128)(2,1)}), bf16[4,64,768]{2,1,0:T(8,128)(2,1)S(1)}, u32[]{:S(2)}, u32[]{:S(2)}) %all-to-all-start.5) | async-done | bytes 393248 | tf_op jit(solution)/shard_map/all_to_all | solution.py:63
  161.3 0.9 maximum_bitcast_fusion
  (45 shorter events, 5.2 us)
Async XLA Ops:
  0.0 71.4 %copy-start = (bf16[1,768,2]{1,2,0:T(2,128)(2,1)S(1)}, bf16[1,768,2]{1,2,0:T(2,128)(2,1)}, u32[]{:S(2)}) copy-start(bf16[1,768,2]{1,2,0:T(2,128)(2,1)} %param.11) | copy-start | bytes 9220
  0.0 64.1 %collective-permute-start.1 = (bf16[768,768]{1,0:T(8,128)(2,1)}, bf16[768,768]{1,0:T(8,128)(2,1)}, u32[]{:S(2)}, u32[]{:S(2)}) collective-permute-start(bf16[768,768]{1,0:T(8,128)(2,1)} %bitcast.110), channel_id=1, source_target_pairs={{0,4},{4,0},{8,12},{12,8},{1,5},{5,1},{9,13},{13,9},{2,6},{6,2},{1... | collective-permute-start | bytes 3538952 | tf_op jit(solution)/shard_map/ppermute | solution.py:10
  3.1 59.3 %copy-start.3 = (bf16[1,1,768,768]{3,2,1,0:T(8,128)(2,1)S(1)}, bf16[1,1,768,768]{3,2,1,0:T(8,128)(2,1)}, u32[]{:S(2)}) copy-start(bf16[1,1,768,768]{3,2,1,0:T(8,128)(2,1)} %param.13) | copy-start | bytes 3538948
  3.1 59.3 %copy-start.4 = (bf16[1,1,768,768]{3,2,1,0:T(8,128)(2,1)S(1)}, bf16[1,1,768,768]{3,2,1,0:T(8,128)(2,1)}, u32[]{:S(2)}) copy-start(bf16[1,1,768,768]{3,2,1,0:T(8,128)(2,1)} %param.12) | copy-start | bytes 3538948
  3.1 61.1 %collective-permute-start = (bf16[768,768]{1,0:T(8,128)(2,1)}, bf16[768,768]{1,0:T(8,128)(2,1)}, u32[]{:S(2)}, u32[]{:S(2)}) collective-permute-start(bf16[768,768]{1,0:T(8,128)(2,1)} %bitcast.111), channel_id=1, source_target_pairs={{0,4},{4,0},{8,12},{12,8},{1,5},{5,1},{9,13},{13,9},{2,6},{6,2},{1... | collective-permute-start | bytes 3538952 | tf_op jit(solution)/shard_map/ppermute | solution.py:10
  64.1 7.2 %copy-start.1 = (bf16[1,128,768]{2,1,0:T(8,128)(2,1)S(1)}, bf16[1,128,768]{2,1,0:T(8,128)(2,1)}, u32[]{:S(2)}) copy-start(bf16[1,128,768]{2,1,0:T(8,128)(2,1)} %param.7) | copy-start | bytes 589828
  67.7 16.9 %copy-start.2 = (bf16[2,128,768]{2,1,0:T(8,128)(2,1)S(1)}, bf16[2,128,768]{2,1,0:T(8,128)(2,1)}, u32[]{:S(2)}) copy-start(bf16[2,128,768]{2,1,0:T(8,128)(2,1)} %param.8) | copy-start | bytes 1179652
  67.7 14.3 %all-to-all-start.1 = ((bf16[4,64,768]{2,1,0:T(8,128)(2,1)}), bf16[4,64,768]{2,1,0:T(8,128)(2,1)S(1)}, u32[]{:S(2)}, u32[]{:S(2)}) async-start(bf16[4,64,768]{2,1,0:T(8,128)(2,1)} %fusion.16), calls=%async_computation.1 | async-start | bytes 786432 | tf_op jit(solution)/shard_map/all_to_all | solution.py:63
  82.2 2.4 %collective-permute-start.2 = (bf16[128,768]{1,0:T(8,128)(2,1)S(1)}, bf16[128,768]{1,0:T(8,128)(2,1)S(1)}, u32[]{:S(2)}, u32[]{:S(2)}) collective-permute-start(bf16[128,768]{1,0:T(8,128)(2,1)S(1)} %fusion.41), channel_id=1, source_target_pairs={{0,1},{1,2},{2,3},{4,5},{5,6},{6,7},{8,9},{9,10},{10,11},{12,13},{... | collective-permute-start | bytes 589832 | tf_op jit(solution)/shard_map/ppermute | solution.py:16
  103.5 16.8 %all-to-all-start.3 = ((bf16[4,64,768]{2,1,0:T(8,128)(2,1)}), bf16[4,64,768]{2,1,0:T(8,128)(2,1)S(1)}, u32[]{:S(2)}, u32[]{:S(2)}) async-start(bf16[4,64,768]{2,1,0:T(8,128)(2,1)} %fusion.12), calls=%async_computation.3 | async-start | bytes 786432 | tf_op jit(solution)/shard_map/all_to_all | solution.py:63
  120.6 3.4 %collective-permute-start.3 = (bf16[128,768]{1,0:T(8,128)(2,1)S(1)}, bf16[128,768]{1,0:T(8,128)(2,1)S(1)}, u32[]{:S(2)}, u32[]{:S(2)}) collective-permute-start(bf16[128,768]{1,0:T(8,128)(2,1)S(1)} %fusion.40), channel_id=1, source_target_pairs={{0,1},{1,2},{2,3},{4,5},{5,6},{6,7},{8,9},{9,10},{10,11},{12,13},{... | collective-permute-start | bytes 589832 | tf_op jit(solution)/shard_map/ppermute | solution.py:16
  145.2 15.8 %all-to-all-start.5 = ((bf16[4,64,768]{2,1,0:T(8,128)(2,1)}), bf16[4,64,768]{2,1,0:T(8,128)(2,1)S(1)}, u32[]{:S(2)}, u32[]{:S(2)}) async-start(bf16[4,64,768]{2,1,0:T(8,128)(2,1)} %fusion.8), calls=%async_computation.5 | async-start | bytes 786432 | tf_op jit(solution)/shard_map/all_to_all | solution.py:63
where the time goes:
time: 163 us; the launch traced here: 162 us
  blocking collectives  81.6 us (50%)
  waiting for transfers between devices  36.7 us (23%)
  matrix products  19.6 us (12%)
  starting transfers between devices  18.3 us (11%)
  other arithmetic  4.56 us (3%)
    all_to_all x3, blocking collectives, expert_layer(): lax.all_to_all(halves, 'expert', split_axis=0, concat_axis=0, tiled=True)  81.6 us
    all_to_all x3, waiting for transfers between devices, expert_layer(): lax.all_to_all(summed, 'expert', split_axis=0, concat_axis=0, tiled=True)  34.6 us
    dot_general x6, matrix products, half_output(): jnp.einsum('sih,hd->sid', hidden, down_projection_matrix, preferred_eleme...  16.3 us
    all_to_all x3, starting transfers between devices, expert_layer(): lax.all_to_all(summed, 'expert', split_axis=0, concat_axis=0, tiled=True)  11.5 us
    ppermute x2, starting transfers between devices, from_behind(): lax.ppermute(value, axis, [(source, source + steps) for source in range(i...  3.64 us
  transfers between devices with their start and end apart: 7, of which 5 were waited for; matrix products, arithmetic and copies ran while one was open for 5% of the time, Pallas kernels for 0%

commit v1 on v0

--- a/solution.py
+++ b/solution.py
@@ -1,7 +1,12 @@
+import functools
+
 import jax
 import jax.numpy as jnp
 from jax import lax
+from jax.experimental import pallas as pl
+from jax.experimental.pallas import tpu as pltpu
 from jax.sharding import PartitionSpec as P
+
 
 TICKS = 3
 
@@ -68,7 +73,7 @@
     return (float_rows + gate_value[:, None] * expert_out).astype(jnp.bfloat16)
 
 
-def per_device(
+def slots_per_device(
     pending_microgroups,
     arriving_microgroups,
     expert_choice_grid,
@@ -101,6 +106,293 @@
     return jnp.stack(per_tick)[None]
 
 
+def piece_list(width):
+    direct = width // 8
+    pieces = []
+    for m, share in ((0, width // 2), (1, (width - direct) // 2)):
+        pieces += [(m, r * (share // 3), share // 3, share) for r in range(3)]
+    return [*pieces, (1, width - direct, direct, 0)]
+
+
+def cut_kernel(some, *refs):
+    count = len(some)
+    sources, outs, sems = refs[: -count - 1], refs[-count - 1 : -1], refs[-1]
+    group = lax.axis_index("groups")
+    copies = []
+    for index, ((m, first, size, share), out) in enumerate(zip(some, outs)):
+        rows = pl.ds(pl.multiple_of(group * share + first, 16), size)
+        copies.append(pltpu.make_async_copy(sources[m].at[rows, :], out, sems.at[index]))
+    for copy in copies:
+        copy.start()
+    for copy in copies:
+        copy.wait()
+
+
+def join_kernel(some, *refs):
+    refs, out_ref = list(refs[:-1]), refs[-1]
+    group = lax.axis_index("groups")
+    for _, first, size, share in some:
+        for part in (group, 1 - group) if share else (0,):
+            rows = pl.ds(pl.multiple_of(part * share + first, 16), size)
+            out_ref[rows, :] = refs.pop(0)[...]
+
+
+HOT_0, OWN_FIRST, WAS_HOT, IS_HOT, FLIP_IN, FLIP_OUT, HOT_2, FLIP_2 = range(8)
+
+
+def table_kernel(here_ref, next_ref, second_ref, behind_ref, table_ref):
+    side = lax.axis_index("expert") // 2
+    leg = lax.axis_index("section")
+    legs = lax.axis_size("section")
+
+    def differ(one, other):
+        return (one != other).astype(jnp.int32)
+
+    def hot(ref, tick):
+        return ref[tick, 0, 0]
+
+    flip_in = differ(hot(here_ref, 0), hot(next_ref, 1))
+    flip_out = jnp.where(leg == legs - 2, 0, differ(hot(next_ref, 1), hot(second_ref, 2)))
+    table_ref[HOT_0] = 1 - differ(hot(here_ref, 0), side)
+    table_ref[OWN_FIRST] = flip_in * (1 - flip_out)
+    table_ref[WAS_HOT] = 1 - differ(hot(behind_ref, 0), side)
+    table_ref[IS_HOT] = 1 - differ(hot(here_ref, 1), side)
+    table_ref[FLIP_IN] = differ(hot(behind_ref, 0), hot(here_ref, 1))
+    table_ref[FLIP_OUT] = jnp.where(
+        leg == legs - 1, 0, differ(hot(here_ref, 1), hot(next_ref, 2))
+    )
+    table_ref[HOT_2] = 1 - differ(hot(here_ref, 2), side)
+    table_ref[FLIP_2] = jnp.where(leg == 0, 0, differ(hot(behind_ref, 1), hot(here_ref, 2)))
+
+
+def expert_rows(x, gain_ref, columns_ref, up_ref, down_ref, far_up_ref, far_down_ref):
+    x = x.astype(jnp.float32)
+    inv_rms = lax.rsqrt(jnp.mean(x * x, axis=-1, keepdims=True) + 1e-06)
+    normed = (x * inv_rms * gain_ref[...]).astype(jnp.bfloat16)
+    columns = columns_ref[...].astype(jnp.float32)
+    column = jnp.where(lax.axis_index("expert") // 2 == 0, columns[0:1], columns[1:2])
+    logit = jnp.sum(normed.astype(jnp.float32) * column, axis=-1, keepdims=True)
+    out = 0.0
+    for into, outof in ((up_ref, down_ref), (far_up_ref, far_down_ref)):
+        up = jnp.dot(normed, into[...], preferred_element_type=jnp.float32)
+        hidden = jnp.maximum(up, 0.0).astype(jnp.bfloat16)
+        out += jnp.dot(hidden, outof[...], preferred_element_type=jnp.float32)
+    return (x + jax.nn.sigmoid(logit) * out).astype(jnp.bfloat16)
+
+
+def choose(flag, one, other):
+    return jnp.where(flag, one, other)
+
+
+def at_first():
+    return lax.axis_index("section") == 0
+
+
+def tick_0(half, table_ref, own_ref, partner_ref, fresh_ref, *refs):
+    *weights, _, both_ref, sent_ref = refs
+    size = sent_ref.shape[0]
+    rows = pl.ds(half * size, size)
+    y = expert_rows(jnp.concatenate([own_ref[rows], partner_ref[rows]]), *weights)
+    both_ref[...] = y
+    last = lax.axis_index("section") == lax.axis_size("section") - 1
+    own = choose(last, fresh_ref[0, rows], y[:size])
+    partner_first = (table_ref[HOT_0] != 0) & (table_ref[OWN_FIRST] == 0)
+    sent_ref[...] = choose(partner_first, y[size:], own)
+
+
+def tick_1_before(half, table_ref, straight_ref, first_ref, fresh_ref, *refs):
+    *weights, _, y_ref, sent_ref = refs
+    size = sent_ref.shape[0]
+    flip_in, flip_out = table_ref[FLIP_IN] != 0, table_ref[FLIP_OUT] != 0
+    own, partner, first = straight_ref[:size], straight_ref[size:], first_ref[...]
+    fresh = fresh_ref[0, pl.ds(half * size, size)]
+    own_in = choose(at_first(), fresh, choose(flip_in, first, own))
+    partner_in = choose(flip_in | at_first(), first, partner)
+    y = expert_rows(choose(flip_out, own_in, partner_in), *weights)
+    y_ref[...] = y
+    waiting = choose(flip_out, choose(at_first(), fresh, own), partner)
+    sent_ref[...] = choose(table_ref[IS_HOT] != 0, y, waiting)
+
+
+def tick_1_after(
+    half, table_ref, straight_ref, first_ref, second_ref, done_ref, fresh_ref, *refs
+):
+    *weights, _, both_ref, was_ref, is_ref = refs
+    size = was_ref.shape[0]
+    flip_in, flip_out = table_ref[FLIP_IN] != 0, table_ref[FLIP_OUT] != 0
+    is_hot = table_ref[IS_HOT] != 0
+    own, partner = straight_ref[:size], straight_ref[size:]
+    first, second, done = first_ref[...], second_ref[...], done_ref[...]
+    fresh = fresh_ref[0, pl.ds(half * size, size)]
+    partner_in = choose(flip_in, second, choose(at_first(), first, partner))
+    own_in = choose(at_first(), fresh, choose(flip_in, second, own))
+    y = expert_rows(choose(flip_out, partner_in, own_in), *weights)
+    both_ref[:size] = choose(is_hot, done, second)
+    both_ref[size:] = y
+    arrived = choose(flip_in & ~flip_out, second, first)
+    was_ref[...] = choose(table_ref[WAS_HOT] != 0, own, arrived)
+    is_ref[...] = choose(is_hot, choose(flip_out, done, y), second)
+
+
+def tick_2_before(half, table_ref, straight_ref, fresh_ref, *refs):
+    *weights, _, sent_ref = refs
+    size = sent_ref.shape[0]
+    fresh = fresh_ref[pl.ds(half * size, size)]
+    y = expert_rows(choose(at_first(), fresh, straight_ref[:size]), *weights)
+    sent_ref[...] = choose(table_ref[HOT_2] != 0, y, straight_ref[size:])
+
+
+def tick_2_after(half, table_ref, straight_ref, third_ref, fresh_ref, *refs):
+    *weights, _, out_ref = refs
+    size = out_ref.shape[0]
+    third = third_ref[...]
+    fresh = fresh_ref[1, pl.ds(half * size, size)]
+    x = choose(table_ref[FLIP_2] != 0, third, straight_ref[size:])
+    y = expert_rows(choose(at_first(), fresh, x), *weights)
+    out_ref[...] = choose(table_ref[HOT_2] != 0, y, third)
+
+
+def gather_kernel(table_ref, *refs):
+    *refs, out_ref = refs
+    size = refs[0].shape[0]
+    late = (table_ref[FLIP_OUT] != 0) & (table_ref[IS_HOT] == 0)
+    for half, (was, here, back, last) in enumerate(zip(*[iter(refs)] * 4)):
+        rows = pl.ds(half * size, size)
+        out_ref[0, 0, rows] = was[...]
+        out_ref[0, 1, rows] = choose(late, back[...], here[...])
+        out_ref[0, 2, rows] = last[...]
+
+
+def pairs_per_device(
+    pending_microgroups,
+    arriving_microgroups,
+    expert_choice_grid,
+    rootmean_gain,
+    gating_columns,
+    up_projection_matrix,
+    down_projection_matrix,
+):
+    places = lax.axis_size("expert")
+    legs = lax.axis_size("section")
+    own = (up_projection_matrix[0, 0], down_projection_matrix[0, 0])
+    width, hid = own[0].shape
+    num_rows = pending_microgroups.shape[1]
+    size = num_rows // 2
+    pieces = piece_list(width)
+    in_vmem = pl.BlockSpec(memory_space=pltpu.VMEM)
+    in_smem = pl.BlockSpec(memory_space=pltpu.SMEM)
+    anywhere = pl.BlockSpec(memory_space=pl.ANY)
+    limited = pltpu.CompilerParams(vmem_limit_bytes=8 << 20)
+
+    def rows_of(count):
+        return jax.ShapeDtypeStruct((count, width), jnp.bfloat16)
+
+    def turned(value, axis, steps):
+        count = lax.axis_size(axis)
+        return lax.ppermute(value, axis, [((i + steps) % count, i) for i in range(count)])
+
+    def cut(some):
+        return pl.pallas_call(
+            functools.partial(cut_kernel, some),
+            out_shape=[jax.ShapeDtypeStruct((p[2], hid), jnp.bfloat16) for p in some],
+            in_specs=[anywhere] * 2,
+            out_specs=[in_vmem] * len(some),
+            scratch_shapes=[pltpu.SemaphoreType.DMA((len(some),))],
+            compiler_params=pltpu.CompilerParams(vmem_limit_bytes=60 << 20),
+        )(*own)
+
+    sending = [*cut(pieces[:1]), *cut(pieces[1:])]
+    near = [swapped(piece, "expert", 0) for piece in sending]
+    parts = [
+        [piece, swapped(piece, "groups", 0)] if pieces[i][3] else [piece]
+        for i, piece in enumerate(near)
+    ]
+
+    def join(m):
+        chosen = [i for i, p in enumerate(pieces) if p[0] == m]
+        operands = [part for i in chosen for part in parts[i]]
+        return pl.pallas_call(
+            functools.partial(join_kernel, [pieces[i] for i in chosen]),
+            out_shape=jax.ShapeDtypeStruct((width, hid), jnp.bfloat16),
+            in_specs=[in_vmem] * len(operands),
+            out_specs=in_vmem,
+            compiler_params=limited,
+        )(*operands)
+
+    routes = [expert_choice_grid]
+    routes += [turned(expert_choice_grid, "section", k) for k in (1, 2, legs - 1)]
+    table = pl.pallas_call(
+        table_kernel,
+        out_shape=jax.ShapeDtypeStruct((8,), jnp.int32),
+        in_specs=[in_smem] * 4,
+        out_specs=in_smem,
+        compiler_params=limited,
+        name="table",
+    )(*routes)
+
+    columns = jnp.swapaxes(gating_columns[0], 0, 1)
+    weights = [rootmean_gain, columns, *own, join(0), join(1)]
+    own_rows = pending_microgroups[0]
+    other_rows = swapped(own_rows, "expert", 1)
+    pairs = [(e * legs, (e ^ 2) * legs) for e in range(places)]
+    fresh_other = lax.ppermute(arriving_microgroups[1], ("expert", "section"), pairs)
+
+    after = [own_rows]
+
+    def stage(body, half, inputs, outs):
+        operands = [table, *inputs, *weights]
+        got = pl.pallas_call(
+            functools.partial(body, half),
+            out_shape=[rows_of(count) for count in outs],
+            in_specs=[in_smem, *[in_vmem] * (len(operands) - 1), anywhere],
+            out_specs=[in_vmem] * len(outs),
+            compiler_params=pltpu.CompilerParams(vmem_limit_bytes=16 << 20),
+        )(*operands, after[-1])
+        after.append(got[0])
+        return got
+
+    def ahead(value, flip, wrap):
+        last = legs if wrap else legs - 1
+        perm = [
+            (e * legs + s, (e ^ flip) * legs + (s + 1) % legs)
+            for e in range(places)
+            for s in range(last)
+        ]
+        return lax.ppermute(value, ("expert", "section"), perm)
+
+    halves = (0, 1)
+    straight, first, second, third = [None] * 2, [None] * 2, [None] * 2, [None] * 2
+    done, was, here, back, last = [None] * 2, [None] * 2, [None] * 2, [None] * 2, [None] * 2
+    for h in halves:
+        both, sent = stage(tick_0, h, [own_rows, other_rows, arriving_microgroups], (2 * size, size))
+        first[h] = ahead(sent, 2, True)
+        straight[h] = ahead(both, 0, True)
+    for h in halves:
+        inputs = [straight[h], first[h], arriving_microgroups]
+        done[h], sent = stage(tick_1_before, h, inputs, (size, size))
+        second[h] = swapped(sent, "expert", 1)
+    for h in halves:
+        inputs = [straight[h], first[h], second[h], done[h], arriving_microgroups]
+        both, was[h], here[h] = stage(tick_1_after, h, inputs, (2 * size, size, size))
+        straight[h] = ahead(both, 0, False)
+        was[h] = turned(was[h], "section", 1)
+    for h in halves:
+        (sent,) = stage(tick_2_before, h, [straight[h], fresh_other], (size,))
+        third[h] = swapped(sent, "expert", 1)
+    for h in halves:
+        back[h] = turned(third[h], "section", 1)
+        (last[h],) = stage(tick_2_after, h, [straight[h], third[h], arriving_microgroups], (size,))
+    operands = [part for h in halves for part in (was[h], here[h], back[h], last[h])]
+    return pl.pallas_call(
+        gather_kernel,
+        out_shape=jax.ShapeDtypeStruct((1, TICKS, num_rows, width), jnp.bfloat16),
+        in_specs=[in_smem, *[in_vmem] * len(operands)],
+        out_specs=in_vmem,
+        compiler_params=limited,
+        name="gather",
+    )(table, *operands)
+
+
 def solution(mesh):
     placed = (
         P("section", ("groups", "expert"), None),
@@ -111,6 +403,14 @@
         P("section", "expert", None, None),
         P("section", "expert", None, None),
     )
+
+    paired = mesh.shape["expert"] == 4 and mesh.shape["groups"] == 2 and mesh.shape["section"] > 2
+
+    def per_device(*args):
+        if paired and args[4].shape[2] == 2 and args[5].shape[2] % 768 == 0:
+            return pairs_per_device(*args)
+        return slots_per_device(*args)
+
     return jax.shard_map(
         per_device,
         mesh=mesh,

time: 163 us -> 102 us (0.63)
  blocking collectives: 81.6 us -> 0 us
  starting transfers between devices: 18.3 us -> 45.6 us
  Pallas kernels: 0 us -> 24 us
  matrix products: 19.6 us -> 0 us
  waiting for transfers between devices: 36.7 us -> 30.1 us
  other arithmetic: 4.56 us -> 0 us
    all_to_all x3 -> x0, blocking collectives: 81.6 us -> none  [expert_layer(): lax.all_to_all(halves, 'expert', split_axis=0, concat_axis=0, tiled=True)]
    all_to_all x3 -> x0, waiting for transfers between devices: 34.6 us -> none  [expert_layer(): lax.all_to_all(summed, 'expert', split_axis=0, concat_axis=0, tiled=True)]
    pallas_call x0 -> x16, Pallas kernels: none -> 24 us  [the longest x10 17.2 us: stage(): pl.pallas_call(functools.partial(body, half), out_shape=[rows_of(count) f...]
    ppermute x2 -> x18, starting transfers between devices: 3.14 us -> 27 us  [swapped(): lax.ppermute(x, axis, [(i, i ^ 1 << bit) for i in range(lax.axis_size(axi...]
    dot_general x15 -> x0, matrix products: 19.6 us -> none  [the longest x6 16.3 us: half_output(): jnp.einsum('sih,hd->sid', hidden, down_projection_matrix, preferred_eleme...]
    ppermute x2 -> x18, waiting for transfers between devices: 0.01 us -> 19.1 us  [swapped(): lax.ppermute(x, axis, [(i, i ^ 1 << bit) for i in range(lax.axis_size(axi...]
    ppermute x2 -> x14, starting transfers between devices: 3.64 us -> 18.6 us  [the longest x6 10 us: ahead(): return lax.ppermute(value, ('expert', 'section'), perm)]
    all_to_all x3 -> x0, starting transfers between devices: 11.5 us -> none  [expert_layer(): lax.all_to_all(summed, 'expert', split_axis=0, concat_axis=0, tiled=True)]
  transfers between devices with their start and end apart: 7 -> 32, of which waited for: 5 -> 15; matrix products, arithmetic and copies ran while one was open for 5% -> 0% of each run, Pallas kernels for 0% -> 17%
where the time goes in v1:
time: 102 us
  starting transfers between devices  45.6 us (45%)
  waiting for transfers between devices  30.1 us (30%)
  Pallas kernels  24 us (24%)
  local copies, waits for them, and re-layouts  1.53 us (2%)
    ppermute x18, starting transfers between devices, swapped(): lax.ppermute(x, axis, [(i, i ^ 1 << bit) for i in range(lax.axis_size(axi...  27 us
    ppermute x18, waiting for transfers between devices, swapped(): lax.ppermute(x, axis, [(i, i ^ 1 << bit) for i in range(lax.axis_size(axi...  19.1 us
    pallas_call x10, Pallas kernels, stage(): pl.pallas_call(functools.partial(body, half), out_shape=[rows_of(count) f...  17.2 us
    ppermute x6, starting transfers between devices, ahead(): return lax.ppermute(value, ('expert', 'section'), perm)  10 us
    ppermute x6, waiting for transfers between devices, ahead(): return lax.ppermute(value, ('expert', 'section'), perm)  7.6 us
    ppermute x7, starting transfers between devices, turned(): lax.ppermute(value, axis, [((i + steps) % count, i) for i in range(count)])  6.36 us
    pallas_call x2, Pallas kernels, cut(): pl.pallas_call(functools.partial(cut_kernel, some), out_shape=[jax.ShapeD...  3.97 us
    ppermute x7, waiting for transfers between devices, turned(): lax.ppermute(value, axis, [((i + steps) % count, i) for i in range(count)])  3.4 us
  transfers between devices with their start and end apart: 32, of which 15 were waited for; matrix products, arithmetic and copies ran while one was open for 0% of the time, Pallas kernels for 17%

profile of v1, /device:TPU:0, one launch (start us, length us, event | category | flops | bytes accessed | tf_op | source)
XLA Modules:
  0.0 101.5 jit_solution(13693406604217093789)
XLA Ops:
  0.0 2.4 %shard_map.74 = (bf16[128,768]{1,0:T(8,128)(2,1)}, bf16[128,768]{1,0:T(8,128)(2,1)}, bf16[112,768]{1,0:T(8,128)(2,1)}, bf16[112,768]{1,0:T(8,128)(2,1)}, bf16[11...) custom-call(bf16[768,768]{1,0:T(8,128)(2,1)} %bitcast.8, bf16[768,768]{1,0:T(8,128)(2,1)} %bitcast.20), custom_call_target="tpu_custom_call" | custom-call | tf_op jit(solution)/shard_map/pallas_call | solution.py:295
  2.4 3.1 %collective-permute-start.10 = (bf16[112,768]{1,0:T(8,128)(2,1)}, bf16[112,768]{1,0:T(8,128)(2,1)S(1)}, u32[]{:S(2)}, u32[]{:S(2)}) collective-permute-start(bf16[112,768]{1,0:T(8,128)(2,1)} %get-tuple-element.27), channel_id=1, source_target_pairs={{0,4},{4,0},{8,12},{12,8},{1,5},{5,1},{9,13},{13,9},{2,6},{6,2},{1... | collective-permute-start | bytes 516104 | tf_op jit(solution)/shard_map/ppermute | solution.py:15
  5.6 1.9 %collective-permute-start.12 = (bf16[112,768]{1,0:T(8,128)(2,1)}, bf16[112,768]{1,0:T(8,128)(2,1)S(1)}, u32[]{:S(2)}, u32[]{:S(2)}) collective-permute-start(bf16[112,768]{1,0:T(8,128)(2,1)} %get-tuple-element.28), channel_id=1, source_target_pairs={{0,4},{4,0},{8,12},{12,8},{1,5},{5,1},{9,13},{13,9},{2,6},{6,2},{1... | collective-permute-start | bytes 516104 | tf_op jit(solution)/shard_map/ppermute | solution.py:15
  10.8 1.9 %collective-permute-done.1.second_ref = s32[3,1,128]{2,1,0:T(1,128)S(1)} collective-permute-done((s32[3,1,128]{2,1,0:T(1,128)S(1)}, s32[3,1,128]{2,1,0:T(1,128)S(1)}, u32[]{:S(2)}, u32[]{:S(2)}) %collective-permute-start.1) | collective-permute-done | bytes 1568 | tf_op jit(solution)/shard_map/ppermute | solution.py:292
  15.7 1.8 %collective-permute-start.6 = (bf16[128,768]{1,0:T(8,128)(2,1)S(1)}, bf16[128,768]{1,0:T(8,128)(2,1)S(1)}, u32[]{:S(2)}, u32[]{:S(2)}) collective-permute-start(bf16[128,768]{1,0:T(8,128)(2,1)S(1)} %copy-done.8), channel_id=1, source_target_pairs={{0,4},{4,0},{8,12},{12,8},{1,5},{5,1},{9,13},{13,9},{2,6},{6,2},{1... | collective-permute-start | bytes 589832 | tf_op jit(solution)/shard_map/ppermute | solution.py:15
  17.7 1.8 %collective-permute-start.4 = (bf16[128,768]{1,0:T(8,128)(2,1)}, bf16[128,768]{1,0:T(8,128)(2,1)S(1)}, u32[]{:S(2)}, u32[]{:S(2)}) collective-permute-start(bf16[128,768]{1,0:T(8,128)(2,1)} %shard_map.73), channel_id=1, source_target_pairs={{0,4},{4,0},{8,12},{12,8},{1,5},{5,1},{9,13},{13,9},{2,6},{6,2},{1... | collective-permute-start | bytes 589832 | tf_op jit(solution)/shard_map/ppermute | solution.py:15
  21.5 2.0 %collective-permute-start.13 = (bf16[112,768]{1,0:T(8,128)(2,1)S(1)}, bf16[112,768]{1,0:T(8,128)(2,1)S(1)}, u32[]{:S(2)}, u32[]{:S(2)}) collective-permute-start(bf16[112,768]{1,0:T(8,128)(2,1)S(1)} %collective-permute-done.12.refs_2_), channel_id=1, source_target_pairs={{0,16},{16,0},{1,17},{17,1},{2,18},{18,2},{3,19},{19,3},{4,20},{20... | collective-permute-start | bytes 516104 | tf_op jit(solution)/shard_map/ppermute | solution.py:15
  23.4 2.2 %collective-permute-done.6.refs_2_ = bf16[128,768]{1,0:T(8,128)(2,1)S(1)} collective-permute-done((bf16[128,768]{1,0:T(8,128)(2,1)S(1)}, bf16[128,768]{1,0:T(8,128)(2,1)S(1)}, u32[]{:S(2)}, u32[]{:S(2)}) %collective-permute-start.6) | collective-permute-done | bytes 196640 | tf_op jit(solution)/shard_map/ppermute | solution.py:15
  25.7 2.0 %collective-permute-start.7 = (bf16[128,768]{1,0:T(8,128)(2,1)S(1)}, bf16[128,768]{1,0:T(8,128)(2,1)S(1)}, u32[]{:S(2)}, u32[]{:S(2)}) collective-permute-start(bf16[128,768]{1,0:T(8,128)(2,1)S(1)} %collective-permute-done.6.refs_2_), channel_id=1, source_target_pairs={{0,16},{16,0},{1,17},{17,1},{2,18},{18,2},{3,19},{19,3},{4,20},{20... | collective-permute-start | bytes 589832 | tf_op jit(solution)/shard_map/ppermute | solution.py:15
  27.6 2.2 %collective-permute-done.8.refs_4_ = bf16[128,768]{1,0:T(8,128)(2,1)S(1)} collective-permute-done((bf16[128,768]{1,0:T(8,128)(2,1)S(1)}, bf16[128,768]{1,0:T(8,128)(2,1)S(1)}, u32[]{:S(2)}, u32[]{:S(2)}) %collective-permute-start.8) | collective-permute-done | bytes 196640 | tf_op jit(solution)/shard_map/ppermute | solution.py:15
  29.9 2.0 %collective-permute-start.9 = (bf16[128,768]{1,0:T(8,128)(2,1)S(1)}, bf16[128,768]{1,0:T(8,128)(2,1)S(1)}, u32[]{:S(2)}, u32[]{:S(2)}) collective-permute-start(bf16[128,768]{1,0:T(8,128)(2,1)S(1)} %collective-permute-done.8.refs_4_), channel_id=1, source_target_pairs={{0,16},{16,0},{1,17},{17,1},{2,18},{18,2},{3,19},{19,3},{4,20},{20... | collective-permute-start | bytes 589832 | tf_op jit(solution)/shard_map/ppermute | solution.py:15
  34.9 2.6 %collective-permute-start.3 = (bf16[128,768]{1,0:T(8,128)(2,1)S(1)}, bf16[128,768]{1,0:T(8,128)(2,1)S(1)}, u32[]{:S(2)}, u32[]{:S(2)}) collective-permute-start(bf16[128,768]{1,0:T(8,128)(2,1)S(1)} %bitcast.32), channel_id=1, source_target_pairs={{0,8},{4,12},{8,0},{12,4},{1,9},{5,13},{9,1},{13,5},{2,10},{6,14},... | collective-permute-start | bytes 589832 | tf_op jit(solution)/shard_map/ppermute | solution.py:15
  39.3 6.0 %collective-permute-done.15.refs_5_ = bf16[112,768]{1,0:T(8,128)(2,1)S(1)} collective-permute-done((bf16[112,768]{1,0:T(8,128)(2,1)S(1)}, bf16[112,768]{1,0:T(8,128)(2,1)S(1)}, u32[]{:S(2)}, u32[]{:S(2)}) %collective-permute-start.15) | collective-permute-done | bytes 172064 | tf_op jit(solution)/shard_map/ppermute | solution.py:15
  51.2 2.3 %collective-permute-start.18 = (bf16[64,768]{1,0:T(8,128)(2,1)S(1)}, bf16[64,768]{1,0:T(8,128)(2,1)S(1)}, u32[]{:S(2)}, u32[]{:S(2)}) collective-permute-start(bf16[64,768]{1,0:T(8,128)(2,1)S(1)} %get-tuple-element.32), channel_id=1, source_target_pairs={{0,9},{1,10},{2,11},{3,8},{4,13},{5,14},{6,15},{7,12},{8,1},{9,2},... | collective-permute-start | bytes 294920 | tf_op jit(solution)/shard_map/ppermute | solution.py:361
  54.8 7.3 %collective-permute-done.18.first_ref = bf16[64,768]{1,0:T(8,128)(2,1)S(1)} collective-permute-done((bf16[64,768]{1,0:T(8,128)(2,1)S(1)}, bf16[64,768]{1,0:T(8,128)(2,1)S(1)}, u32[]{:S(2)}, u32[]{:S(2)}) %collective-permute-start.18) | collective-permute-done | bytes 98336 | tf_op jit(solution)/shard_map/ppermute | solution.py:361
  65.9 2.7 %collective-permute-start.25 = (bf16[64,768]{1,0:T(8,128)(2,1)S(1)}, bf16[64,768]{1,0:T(8,128)(2,1)S(1)}, u32[]{:S(2)}, u32[]{:S(2)}) collective-permute-start(bf16[64,768]{1,0:T(8,128)(2,1)S(1)} %get-tuple-element.41), channel_id=1, source_target_pairs={{0,8},{4,12},{8,0},{12,4},{1,9},{5,13},{9,1},{13,5},{2,10},{6,14},... | collective-permute-start | bytes 294920 | tf_op jit(solution)/shard_map/ppermute | solution.py:15
  68.6 2.2 %collective-permute-start.24 = (bf16[128,768]{1,0:T(8,128)(2,1)S(1)}, bf16[128,768]{1,0:T(8,128)(2,1)S(1)}, u32[]{:S(2)}, u32[]{:S(2)}) collective-permute-start(bf16[128,768]{1,0:T(8,128)(2,1)S(1)} %slice_bitcast_fusion), channel_id=1, source_target_pairs={{0,8},{4,12},{8,0},{12,4},{16,24},{20,28},{24,16},{28,20}} | collective-permute-start | bytes 589832 | tf_op jit(solution)/shard_map/ppermute | solution.py:338
  76.7 4.4 %collective-permute-start.28 = (bf16[128,768]{1,0:T(8,128)(2,1)S(1)}, bf16[128,768]{1,0:T(8,128)(2,1)S(1)}, u32[]{:S(2)}, u32[]{:S(2)}) collective-permute-start(bf16[128,768]{1,0:T(8,128)(2,1)S(1)} %get-tuple-element.42.refs_6_), channel_id=1, source_target_pairs={{0,1},{1,2},{2,3},{4,5},{5,6},{6,7},{8,9},{9,10},{10,11},{12,13},{... | collective-permute-start | bytes 589832 | tf_op jit(solution)/shard_map/ppermute | solution.py:361
  81.2 1.7 %shard_map.83.refs_6_ = bf16[64,768]{1,0:T(8,128)(2,1)S(1)} custom-call(s32[8]{0:T(128)S(1)} %table.1.table_ref, bf16[128,768]{1,0:T(8,128)(2,1)S(1)} %collective-permute-done.23.straight_ref, bf16[128,768]{1,0:T(8,128)(2,1)S(1)} %collective-permute-done.24.fresh_ref, f32[1,768]{1,0:T(1,128)S(1)} %copy-done.4, bf16[2,768]{1,0:T(2,128)(2,1)S(1)} %bitcast.42, ...), custom_call_target="tpu_custom_call" | custom-call | tf_op jit(solution)/shard_map/pallas_call | solution.py:344
  83.0 1.7 %shard_map.84.refs_6_ = bf16[64,768]{1,0:T(8,128)(2,1)S(1)} custom-call(s32[8]{0:T(128)S(1)} %table.1.table_ref, bf16[128,768]{1,0:T(8,128)(2,1)S(1)} %collective-permute-done.28.straight_ref, bf16[128,768]{1,0:T(8,128)(2,1)S(1)} %collective-permute-done.24.fresh_ref, f32[1,768]{1,0:T(1,128)S(1)} %copy-done.4, bf16[2,768]{1,0:T(2,128)(2,1)S(1)} %bitcast.43, ...), custom_call_target="tpu_custom_call" | custom-call | tf_op jit(solution)/shard_map/pallas_call | solution.py:344
  84.8 2.9 %collective-permute-start.26 = (bf16[64,768]{1,0:T(8,128)(2,1)S(1)}, bf16[64,768]{1,0:T(8,128)(2,1)S(1)}, u32[]{:S(2)}, u32[]{:S(2)}) collective-permute-start(bf16[64,768]{1,0:T(8,128)(2,1)S(1)} %shard_map.83.refs_6_), channel_id=1, source_target_pairs={{0,8},{4,12},{8,0},{12,4},{1,9},{5,13},{9,1},{13,5},{2,10},{6,14},... | collective-permute-start | bytes 294920 | tf_op jit(solution)/shard_map/ppermute | solution.py:15
  87.7 3.3 %collective-permute-start.22 = (bf16[64,768]{1,0:T(8,128)(2,1)S(1)}, bf16[64,768]{1,0:T(8,128)(2,1)S(1)}, u32[]{:S(2)}, u32[]{:S(2)}) collective-permute-start(bf16[64,768]{1,0:T(8,128)(2,1)S(1)} %get-tuple-element.38), channel_id=1, source_target_pairs={{1,0},{2,1},{3,2},{0,3},{5,4},{6,5},{7,6},{4,7},{9,8},{10,9},{11,1... | collective-permute-start | bytes 294920 | tf_op jit(solution)/shard_map/ppermute | solution.py:292
  91.0 3.5 %collective-permute-done.30.third_ref = bf16[64,768]{1,0:T(8,128)(2,1)S(1)} collective-permute-done((bf16[64,768]{1,0:T(8,128)(2,1)S(1)}, bf16[64,768]{1,0:T(8,128)(2,1)S(1)}, u32[]{:S(2)}, u32[]{:S(2)}) %collective-permute-start.30) | collective-permute-done | bytes 98336 | tf_op jit(solution)/shard_map/ppermute | solution.py:15
  94.5 2.1 %collective-permute-done.26.third_ref = bf16[64,768]{1,0:T(8,128)(2,1)S(1)} collective-permute-done((bf16[64,768]{1,0:T(8,128)(2,1)S(1)}, bf16[64,768]{1,0:T(8,128)(2,1)S(1)}, u32[]{:S(2)}, u32[]{:S(2)}) %collective-permute-start.26) | collective-permute-done | bytes 98336 | tf_op jit(solution)/shard_map/ppermute | solution.py:15
  (75 shorter events, 35.3 us)
Async XLA Ops:
  2.4 15.3 %collective-permute-start.10 = (bf16[112,768]{1,0:T(8,128)(2,1)}, bf16[112,768]{1,0:T(8,128)(2,1)S(1)}, u32[]{:S(2)}, u32[]{:S(2)}) collective-permute-start(bf16[112,768]{1,0:T(8,128)(2,1)} %get-tuple-element.27), channel_id=1, source_target_pairs={{0,4},{4,0},{8,12},{12,8},{1,5},{5,1},{9,13},{13,9},{2,6},{6,2},{1... | collective-permute-start | bytes 516104 | tf_op jit(solution)/shard_map/ppermute | solution.py:15
  5.5 12.0 %collective-permute-start.16 = (bf16[96,768]{1,0:T(8,128)(2,1)}, bf16[96,768]{1,0:T(8,128)(2,1)S(1)}, u32[]{:S(2)}, u32[]{:S(2)}) collective-permute-start(bf16[96,768]{1,0:T(8,128)(2,1)} %get-tuple-element.30), channel_id=1, source_target_pairs={{0,4},{4,0},{8,12},{12,8},{1,5},{5,1},{9,13},{13,9},{2,6},{6,2},{1... | collective-permute-start | bytes 442376 | tf_op jit(solution)/shard_map/ppermute | solution.py:15
  5.6 13.9 %collective-permute-start.12 = (bf16[112,768]{1,0:T(8,128)(2,1)}, bf16[112,768]{1,0:T(8,128)(2,1)S(1)}, u32[]{:S(2)}, u32[]{:S(2)}) collective-permute-start(bf16[112,768]{1,0:T(8,128)(2,1)} %get-tuple-element.28), channel_id=1, source_target_pairs={{0,4},{4,0},{8,12},{12,8},{1,5},{5,1},{9,13},{13,9},{2,6},{6,2},{1... | collective-permute-start | bytes 516104 | tf_op jit(solution)/shard_map/ppermute | solution.py:15
  7.5 13.9 %collective-permute-start.14 = (bf16[112,768]{1,0:T(8,128)(2,1)}, bf16[112,768]{1,0:T(8,128)(2,1)S(1)}, u32[]{:S(2)}, u32[]{:S(2)}) collective-permute-start(bf16[112,768]{1,0:T(8,128)(2,1)} %get-tuple-element.29), channel_id=1, source_target_pairs={{0,4},{4,0},{8,12},{12,8},{1,5},{5,1},{9,13},{13,9},{2,6},{6,2},{1... | collective-permute-start | bytes 516104 | tf_op jit(solution)/shard_map/ppermute | solution.py:15
  15.7 10.0 %collective-permute-start.6 = (bf16[128,768]{1,0:T(8,128)(2,1)S(1)}, bf16[128,768]{1,0:T(8,128)(2,1)S(1)}, u32[]{:S(2)}, u32[]{:S(2)}) collective-permute-start(bf16[128,768]{1,0:T(8,128)(2,1)S(1)} %copy-done.8), channel_id=1, source_target_pairs={{0,4},{4,0},{8,12},{12,8},{1,5},{5,1},{9,13},{13,9},{2,6},{6,2},{1... | collective-permute-start | bytes 589832 | tf_op jit(solution)/shard_map/ppermute | solution.py:15
  17.5 12.4 %collective-permute-start.8 = (bf16[128,768]{1,0:T(8,128)(2,1)S(1)}, bf16[128,768]{1,0:T(8,128)(2,1)S(1)}, u32[]{:S(2)}, u32[]{:S(2)}) collective-permute-start(bf16[128,768]{1,0:T(8,128)(2,1)S(1)} %copy-done.7), channel_id=1, source_target_pairs={{0,4},{4,0},{8,12},{12,8},{1,5},{5,1},{9,13},{13,9},{2,6},{6,2},{1... | collective-permute-start | bytes 589832 | tf_op jit(solution)/shard_map/ppermute | solution.py:15
  17.7 15.5 %collective-permute-start.4 = (bf16[128,768]{1,0:T(8,128)(2,1)}, bf16[128,768]{1,0:T(8,128)(2,1)S(1)}, u32[]{:S(2)}, u32[]{:S(2)}) collective-permute-start(bf16[128,768]{1,0:T(8,128)(2,1)} %shard_map.73), channel_id=1, source_target_pairs={{0,4},{4,0},{8,12},{12,8},{1,5},{5,1},{9,13},{13,9},{2,6},{6,2},{1... | collective-permute-start | bytes 589832 | tf_op jit(solution)/shard_map/ppermute | solution.py:15
  19.5 15.4 %collective-permute-start.11 = (bf16[112,768]{1,0:T(8,128)(2,1)S(1)}, bf16[112,768]{1,0:T(8,128)(2,1)S(1)}, u32[]{:S(2)}, u32[]{:S(2)}) collective-permute-start(bf16[112,768]{1,0:T(8,128)(2,1)S(1)} %collective-permute-done.10.refs_0_), channel_id=1, source_target_pairs={{0,16},{16,0},{1,17},{17,1},{2,18},{18,2},{3,19},{19,3},{4,20},{20... | collective-permute-start | bytes 516104 | tf_op jit(solution)/shard_map/ppermute | solution.py:15
  21.5 16.1 %collective-permute-start.13 = (bf16[112,768]{1,0:T(8,128)(2,1)S(1)}, bf16[112,768]{1,0:T(8,128)(2,1)S(1)}, u32[]{:S(2)}, u32[]{:S(2)}) collective-permute-start(bf16[112,768]{1,0:T(8,128)(2,1)S(1)} %collective-permute-done.12.refs_2_), channel_id=1, source_target_pairs={{0,16},{16,0},{1,17},{17,1},{2,18},{18,2},{3,19},{19,3},{4,20},{20... | collective-permute-start | bytes 516104 | tf_op jit(solution)/shard_map/ppermute | solution.py:15
  25.7 19.7 %collective-permute-start.7 = (bf16[128,768]{1,0:T(8,128)(2,1)S(1)}, bf16[128,768]{1,0:T(8,128)(2,1)S(1)}, u32[]{:S(2)}, u32[]{:S(2)}) collective-permute-start(bf16[128,768]{1,0:T(8,128)(2,1)S(1)} %collective-permute-done.6.refs_2_), channel_id=1, source_target_pairs={{0,16},{16,0},{1,17},{17,1},{2,18},{18,2},{3,19},{19,3},{4,20},{20... | collective-permute-start | bytes 589832 | tf_op jit(solution)/shard_map/ppermute | solution.py:15
  29.9 15.5 %collective-permute-start.9 = (bf16[128,768]{1,0:T(8,128)(2,1)S(1)}, bf16[128,768]{1,0:T(8,128)(2,1)S(1)}, u32[]{:S(2)}, u32[]{:S(2)}) collective-permute-start(bf16[128,768]{1,0:T(8,128)(2,1)S(1)} %collective-permute-done.8.refs_4_), channel_id=1, source_target_pairs={{0,16},{16,0},{1,17},{17,1},{2,18},{18,2},{3,19},{19,3},{4,20},{20... | collective-permute-start | bytes 589832 | tf_op jit(solution)/shard_map/ppermute | solution.py:15
  33.2 12.1 %collective-permute-start.5 = (bf16[128,768]{1,0:T(8,128)(2,1)S(1)}, bf16[128,768]{1,0:T(8,128)(2,1)S(1)}, u32[]{:S(2)}, u32[]{:S(2)}) collective-permute-start(bf16[128,768]{1,0:T(8,128)(2,1)S(1)} %collective-permute-done.4.refs_0_), channel_id=1, source_target_pairs={{0,16},{16,0},{1,17},{17,1},{2,18},{18,2},{3,19},{19,3},{4,20},{20... | collective-permute-start | bytes 589832 | tf_op jit(solution)/shard_map/ppermute | solution.py:15
  34.9 10.6 %collective-permute-start.3 = (bf16[128,768]{1,0:T(8,128)(2,1)S(1)}, bf16[128,768]{1,0:T(8,128)(2,1)S(1)}, u32[]{:S(2)}, u32[]{:S(2)}) collective-permute-start(bf16[128,768]{1,0:T(8,128)(2,1)S(1)} %bitcast.32), channel_id=1, source_target_pairs={{0,8},{4,12},{8,0},{12,4},{1,9},{5,13},{9,1},{13,5},{2,10},{6,14},... | collective-permute-start | bytes 589832 | tf_op jit(solution)/shard_map/ppermute | solution.py:15
  48.8 13.3 %collective-permute-start.17 = (bf16[128,768]{1,0:T(8,128)(2,1)S(1)}, bf16[128,768]{1,0:T(8,128)(2,1)S(1)}, u32[]{:S(2)}, u32[]{:S(2)}) collective-permute-start(bf16[128,768]{1,0:T(8,128)(2,1)S(1)} %get-tuple-element.31.refs_6_), channel_id=1, source_target_pairs={{0,1},{1,2},{2,3},{3,0},{4,5},{5,6},{6,7},{7,4},{8,9},{9,10},{10,1... | collective-permute-start | bytes 589832 | tf_op jit(solution)/shard_map/ppermute | solution.py:361
  50.5 13.7 %collective-permute-start.20 = (bf16[128,768]{1,0:T(8,128)(2,1)S(1)}, bf16[128,768]{1,0:T(8,128)(2,1)S(1)}, u32[]{:S(2)}, u32[]{:S(2)}) collective-permute-start(bf16[128,768]{1,0:T(8,128)(2,1)S(1)} %get-tuple-element.33.refs_6_), channel_id=1, source_target_pairs={{0,1},{1,2},{2,3},{3,0},{4,5},{5,6},{6,7},{7,4},{8,9},{9,10},{10,1... | collective-permute-start | bytes 589832 | tf_op jit(solution)/shard_map/ppermute | solution.py:361
  51.2 10.9 %collective-permute-start.18 = (bf16[64,768]{1,0:T(8,128)(2,1)S(1)}, bf16[64,768]{1,0:T(8,128)(2,1)S(1)}, u32[]{:S(2)}, u32[]{:S(2)}) collective-permute-start(bf16[64,768]{1,0:T(8,128)(2,1)S(1)} %get-tuple-element.32), channel_id=1, source_target_pairs={{0,9},{1,10},{2,11},{3,8},{4,13},{5,14},{6,15},{7,12},{8,1},{9,2},... | collective-permute-start | bytes 294920 | tf_op jit(solution)/shard_map/ppermute | solution.py:361
  53.5 10.7 %collective-permute-start.21 = (bf16[64,768]{1,0:T(8,128)(2,1)S(1)}, bf16[64,768]{1,0:T(8,128)(2,1)S(1)}, u32[]{:S(2)}, u32[]{:S(2)}) collective-permute-start(bf16[64,768]{1,0:T(8,128)(2,1)S(1)} %get-tuple-element.36), channel_id=1, source_target_pairs={{0,9},{1,10},{2,11},{3,8},{4,13},{5,14},{6,15},{7,12},{8,1},{9,2},... | collective-permute-start | bytes 294920 | tf_op jit(solution)/shard_map/ppermute | solution.py:361
  63.8 8.0 %collective-permute-start.19 = (bf16[64,768]{1,0:T(8,128)(2,1)S(1)}, bf16[64,768]{1,0:T(8,128)(2,1)S(1)}, u32[]{:S(2)}, u32[]{:S(2)}) collective-permute-start(bf16[64,768]{1,0:T(8,128)(2,1)S(1)} %get-tuple-element.34), channel_id=1, source_target_pairs={{0,8},{4,12},{8,0},{12,4},{1,9},{5,13},{9,1},{13,5},{2,10},{6,14},... | collective-permute-start | bytes 294920 | tf_op jit(solution)/shard_map/ppermute | solution.py:15
  65.9 9.1 %collective-permute-start.25 = (bf16[64,768]{1,0:T(8,128)(2,1)S(1)}, bf16[64,768]{1,0:T(8,128)(2,1)S(1)}, u32[]{:S(2)}, u32[]{:S(2)}) collective-permute-start(bf16[64,768]{1,0:T(8,128)(2,1)S(1)} %get-tuple-element.41), channel_id=1, source_target_pairs={{0,8},{4,12},{8,0},{12,4},{1,9},{5,13},{9,1},{13,5},{2,10},{6,14},... | collective-permute-start | bytes 294920 | tf_op jit(solution)/shard_map/ppermute | solution.py:15
  68.6 12.6 %collective-permute-start.24 = (bf16[128,768]{1,0:T(8,128)(2,1)S(1)}, bf16[128,768]{1,0:T(8,128)(2,1)S(1)}, u32[]{:S(2)}, u32[]{:S(2)}) collective-permute-start(bf16[128,768]{1,0:T(8,128)(2,1)S(1)} %slice_bitcast_fusion), channel_id=1, source_target_pairs={{0,8},{4,12},{8,0},{12,4},{16,24},{20,28},{24,16},{28,20}} | collective-permute-start | bytes 589832 | tf_op jit(solution)/shard_map/ppermute | solution.py:338
  84.7 9.8 %collective-permute-start.30 = (bf16[64,768]{1,0:T(8,128)(2,1)S(1)}, bf16[64,768]{1,0:T(8,128)(2,1)S(1)}, u32[]{:S(2)}, u32[]{:S(2)}) collective-permute-start(bf16[64,768]{1,0:T(8,128)(2,1)S(1)} %shard_map.84.refs_6_), channel_id=1, source_target_pairs={{0,8},{4,12},{8,0},{12,4},{1,9},{5,13},{9,1},{13,5},{2,10},{6,14},... | collective-permute-start | bytes 294920 | tf_op jit(solution)/shard_map/ppermute | solution.py:15
  84.8 11.8 %collective-permute-start.26 = (bf16[64,768]{1,0:T(8,128)(2,1)S(1)}, bf16[64,768]{1,0:T(8,128)(2,1)S(1)}, u32[]{:S(2)}, u32[]{:S(2)}) collective-permute-start(bf16[64,768]{1,0:T(8,128)(2,1)S(1)} %shard_map.83.refs_6_), channel_id=1, source_target_pairs={{0,8},{4,12},{8,0},{12,4},{1,9},{5,13},{9,1},{13,5},{2,10},{6,14},... | collective-permute-start | bytes 294920 | tf_op jit(solution)/shard_map/ppermute | solution.py:15
  87.7 12.4 %collective-permute-start.29 = (bf16[64,768]{1,0:T(8,128)(2,1)S(1)}, bf16[64,768]{1,0:T(8,128)(2,1)S(1)}, u32[]{:S(2)}, u32[]{:S(2)}) collective-permute-start(bf16[64,768]{1,0:T(8,128)(2,1)S(1)} %get-tuple-element.43), channel_id=1, source_target_pairs={{1,0},{2,1},{3,2},{0,3},{5,4},{6,5},{7,6},{4,7},{9,8},{10,9},{11,1... | collective-permute-start | bytes 294920 | tf_op jit(solution)/shard_map/ppermute | solution.py:292
  87.7 12.4 %collective-permute-start.22 = (bf16[64,768]{1,0:T(8,128)(2,1)S(1)}, bf16[64,768]{1,0:T(8,128)(2,1)S(1)}, u32[]{:S(2)}, u32[]{:S(2)}) collective-permute-start(bf16[64,768]{1,0:T(8,128)(2,1)S(1)} %get-tuple-element.38), channel_id=1, source_target_pairs={{1,0},{2,1},{3,2},{0,3},{5,4},{6,5},{7,6},{4,7},{9,8},{10,9},{11,1... | collective-permute-start | bytes 294920 | tf_op jit(solution)/shard_map/ppermute | solution.py:292
  (17 other events, 98.0 us)

commit v2 on v1

--- a/solution.py
+++ b/solution.py
@@ -137,10 +137,11 @@
             out_ref[rows, :] = refs.pop(0)[...]
 
 
-HOT_0, OWN_FIRST, WAS_HOT, IS_HOT, FLIP_IN, FLIP_OUT, HOT_2, FLIP_2 = range(8)
-
-
-def table_kernel(here_ref, next_ref, second_ref, behind_ref, table_ref):
+PARTNER_FIRST, WAS_HOT, IS_HOT, FLIP_IN, FLIP_OUT, LATE, HOT_2, FLIP_2 = range(8)
+
+
+def table_kernel(here_ref, next_ref, second_ref, behind_ref, *refs):
+    table_ref = refs[-1]
     side = lax.axis_index("expert") // 2
     leg = lax.axis_index("section")
     legs = lax.axis_size("section")
@@ -151,18 +152,23 @@
     def hot(ref, tick):
         return ref[tick, 0, 0]
 
+    def write(row, value):
+        table_ref[row : row + 1] = jnp.full((1, table_ref.shape[1]), value, jnp.int32)
+
     flip_in = differ(hot(here_ref, 0), hot(next_ref, 1))
     flip_out = jnp.where(leg == legs - 2, 0, differ(hot(next_ref, 1), hot(second_ref, 2)))
-    table_ref[HOT_0] = 1 - differ(hot(here_ref, 0), side)
-    table_ref[OWN_FIRST] = flip_in * (1 - flip_out)
-    table_ref[WAS_HOT] = 1 - differ(hot(behind_ref, 0), side)
-    table_ref[IS_HOT] = 1 - differ(hot(here_ref, 1), side)
-    table_ref[FLIP_IN] = differ(hot(behind_ref, 0), hot(here_ref, 1))
-    table_ref[FLIP_OUT] = jnp.where(
-        leg == legs - 1, 0, differ(hot(here_ref, 1), hot(next_ref, 2))
-    )
-    table_ref[HOT_2] = 1 - differ(hot(here_ref, 2), side)
-    table_ref[FLIP_2] = jnp.where(leg == 0, 0, differ(hot(behind_ref, 1), hot(here_ref, 2)))
+    own_first = flip_in * (1 - flip_out)
+    write(PARTNER_FIRST, (1 - differ(hot(here_ref, 0), side)) * (1 - own_first))
+    flip_in = differ(hot(behind_ref, 0), hot(here_ref, 1))
+    flip_out = jnp.where(leg == legs - 1, 0, differ(hot(here_ref, 1), hot(next_ref, 2)))
+    is_hot = 1 - differ(hot(here_ref, 1), side)
+    write(WAS_HOT, 1 - differ(hot(behind_ref, 0), side))
+    write(IS_HOT, is_hot)
+    write(FLIP_IN, flip_in)
+    write(FLIP_OUT, flip_out)
+    write(LATE, flip_out * (1 - is_hot))
+    write(HOT_2, 1 - differ(hot(here_ref, 2), side))
+    write(FLIP_2, jnp.where(leg == 0, 0, differ(hot(behind_ref, 1), hot(here_ref, 2))))
 
 
 def expert_rows(x, gain_ref, columns_ref, up_ref, down_ref, far_up_ref, far_down_ref):
@@ -180,66 +186,81 @@
     return (x + jax.nn.sigmoid(logit) * out).astype(jnp.bfloat16)
 
 
-def choose(flag, one, other):
-    return jnp.where(flag, one, other)
+def flag(table_ref, row):
+    return table_ref[row : row + 1, :1]
+
+
+def choose(chosen, one, other):
+    return jnp.where(chosen != 0, one, other)
 
 
 def at_first():
     return lax.axis_index("section") == 0
 
 
-def tick_0(half, table_ref, own_ref, partner_ref, fresh_ref, *refs):
-    *weights, _, both_ref, sent_ref = refs
-    size = sent_ref.shape[0]
-    rows = pl.ds(half * size, size)
-    y = expert_rows(jnp.concatenate([own_ref[rows], partner_ref[rows]]), *weights)
+def tick_0(table_ref, own_ref, partner_ref, fresh_ref, *refs):
+    *weights, _, both_ref, first_ref, second_ref = refs
+    count, size = own_ref.shape[0], first_ref.shape[0]
+    y = expert_rows(jnp.concatenate([own_ref[...], partner_ref[...]]), *weights)
     both_ref[...] = y
     last = lax.axis_index("section") == lax.axis_size("section") - 1
-    own = choose(last, fresh_ref[0, rows], y[:size])
-    partner_first = (table_ref[HOT_0] != 0) & (table_ref[OWN_FIRST] == 0)
-    sent_ref[...] = choose(partner_first, y[size:], own)
+    own = jnp.where(last, fresh_ref[0], y[:count])
+    sent = choose(flag(table_ref, PARTNER_FIRST), y[count:], own)
+    first_ref[...] = sent[:size]
+    second_ref[...] = sent[size:]
+
+
+def halves_of(straight_ref, half, size):
+    count = straight_ref.shape[0] // 2
+    rows = pl.ds(half * size, size)
+    return straight_ref[rows], straight_ref[pl.ds(count + half * size, size)]
 
 
 def tick_1_before(half, table_ref, straight_ref, first_ref, fresh_ref, *refs):
     *weights, _, y_ref, sent_ref = refs
     size = sent_ref.shape[0]
-    flip_in, flip_out = table_ref[FLIP_IN] != 0, table_ref[FLIP_OUT] != 0
-    own, partner, first = straight_ref[:size], straight_ref[size:], first_ref[...]
+    flip_in, flip_out = flag(table_ref, FLIP_IN), flag(table_ref, FLIP_OUT)
+    own, partner = halves_of(straight_ref, half, size)
+    first = first_ref[...]
     fresh = fresh_ref[0, pl.ds(half * size, size)]
-    own_in = choose(at_first(), fresh, choose(flip_in, first, own))
-    partner_in = choose(flip_in | at_first(), first, partner)
+    own_in = jnp.where(at_first(), fresh, choose(flip_in, first, own))
+    partner_in = jnp.where(at_first(), first, choose(flip_in, first, partner))
     y = expert_rows(choose(flip_out, own_in, partner_in), *weights)
     y_ref[...] = y
-    waiting = choose(flip_out, choose(at_first(), fresh, own), partner)
-    sent_ref[...] = choose(table_ref[IS_HOT] != 0, y, waiting)
-
-
-def tick_1_after(
-    half, table_ref, straight_ref, first_ref, second_ref, done_ref, fresh_ref, *refs
-):
-    *weights, _, both_ref, was_ref, is_ref = refs
-    size = was_ref.shape[0]
-    flip_in, flip_out = table_ref[FLIP_IN] != 0, table_ref[FLIP_OUT] != 0
-    is_hot = table_ref[IS_HOT] != 0
-    own, partner = straight_ref[:size], straight_ref[size:]
-    first, second, done = first_ref[...], second_ref[...], done_ref[...]
+    waiting = choose(flip_out, jnp.where(at_first(), fresh, own), partner)
+    sent_ref[...] = choose(flag(table_ref, IS_HOT), y, waiting)
+
+
+def tick_1_after(half, table_ref, straight_ref, done_ref, fresh_ref, *refs):
+    first_refs, second_refs = refs[: half + 1], refs[half + 1 : 2 * half + 2]
+    *weights, _, both_ref, is_ref = refs[2 * half + 2 : len(refs) - half]
+    size = is_ref.shape[0]
+    flip_in, flip_out = flag(table_ref, FLIP_IN), flag(table_ref, FLIP_OUT)
+    is_hot = flag(table_ref, IS_HOT)
+    own, partner = halves_of(straight_ref, half, size)
+    first, second, done = first_refs[half][...], second_refs[half][...], done_ref[...]
     fresh = fresh_ref[0, pl.ds(half * size, size)]
-    partner_in = choose(flip_in, second, choose(at_first(), first, partner))
-    own_in = choose(at_first(), fresh, choose(flip_in, second, own))
+    partner_in = choose(flip_in, second, jnp.where(at_first(), first, partner))
+    own_in = jnp.where(at_first(), fresh, choose(flip_in, second, own))
     y = expert_rows(choose(flip_out, partner_in, own_in), *weights)
     both_ref[:size] = choose(is_hot, done, second)
     both_ref[size:] = y
-    arrived = choose(flip_in & ~flip_out, second, first)
-    was_ref[...] = choose(table_ref[WAS_HOT] != 0, own, arrived)
     is_ref[...] = choose(is_hot, choose(flip_out, done, y), second)
+    if half:
+        was_ref = refs[-1]
+        swapped_in = flip_in * (1 - flip_out)
+        for part in range(half + 1):
+            own, _ = halves_of(straight_ref, part, size)
+            arrived = choose(swapped_in, second_refs[part][...], first_refs[part][...])
+            was_ref[pl.ds(part * size, size)] = choose(flag(table_ref, WAS_HOT), own, arrived)
 
 
 def tick_2_before(half, table_ref, straight_ref, fresh_ref, *refs):
     *weights, _, sent_ref = refs
     size = sent_ref.shape[0]
     fresh = fresh_ref[pl.ds(half * size, size)]
-    y = expert_rows(choose(at_first(), fresh, straight_ref[:size]), *weights)
-    sent_ref[...] = choose(table_ref[HOT_2] != 0, y, straight_ref[size:])
+    y = expert_rows(jnp.where(at_first(), fresh, straight_ref[:size]), *weights)
+    sent_ref[...] = choose(flag(table_ref, HOT_2), y, straight_ref[size:])
 
 
 def tick_2_after(half, table_ref, straight_ref, third_ref, fresh_ref, *refs):
@@ -247,19 +268,18 @@
     size = out_ref.shape[0]
     third = third_ref[...]
     fresh = fresh_ref[1, pl.ds(half * size, size)]
-    x = choose(table_ref[FLIP_2] != 0, third, straight_ref[size:])
-    y = expert_rows(choose(at_first(), fresh, x), *weights)
-    out_ref[...] = choose(table_ref[HOT_2] != 0, y, third)
-
-
-def gather_kernel(table_ref, *refs):
+    x = choose(flag(table_ref, FLIP_2), third, straight_ref[size:])
+    y = expert_rows(jnp.where(at_first(), fresh, x), *weights)
+    out_ref[...] = choose(flag(table_ref, HOT_2), y, third)
+
+
+def gather_kernel(table_ref, was_ref, *refs):
     *refs, out_ref = refs
     size = refs[0].shape[0]
-    late = (table_ref[FLIP_OUT] != 0) & (table_ref[IS_HOT] == 0)
-    for half, (was, here, back, last) in enumerate(zip(*[iter(refs)] * 4)):
+    out_ref[0, 0] = was_ref[...]
+    for half, (here, back, last) in enumerate(zip(*[iter(refs)] * 3)):
         rows = pl.ds(half * size, size)
-        out_ref[0, 0, rows] = was[...]
-        out_ref[0, 1, rows] = choose(late, back[...], here[...])
+        out_ref[0, 1, rows] = choose(flag(table_ref, LATE), back[...], here[...])
         out_ref[0, 2, rows] = last[...]
 
 
@@ -319,18 +339,18 @@
             compiler_params=limited,
         )(*operands)
 
+    columns = jnp.swapaxes(gating_columns[0], 0, 1)
     routes = [expert_choice_grid]
     routes += [turned(expert_choice_grid, "section", k) for k in (1, 2, legs - 1)]
     table = pl.pallas_call(
         table_kernel,
-        out_shape=jax.ShapeDtypeStruct((8,), jnp.int32),
-        in_specs=[in_smem] * 4,
-        out_specs=in_smem,
+        out_shape=jax.ShapeDtypeStruct((8, 128), jnp.int32),
+        in_specs=[in_smem] * 4 + [in_vmem] * 5,
+        out_specs=in_vmem,
         compiler_params=limited,
         name="table",
-    )(*routes)
-
-    columns = jnp.swapaxes(gating_columns[0], 0, 1)
+    )(*routes, *own, rootmean_gain, columns, arriving_microgroups)
+
     weights = [rootmean_gain, columns, *own, join(0), join(1)]
     own_rows = pending_microgroups[0]
     other_rows = swapped(own_rows, "expert", 1)
@@ -342,9 +362,9 @@
     def stage(body, half, inputs, outs):
         operands = [table, *inputs, *weights]
         got = pl.pallas_call(
-            functools.partial(body, half),
+            body if half is None else functools.partial(body, half),
             out_shape=[rows_of(count) for count in outs],
-            in_specs=[in_smem, *[in_vmem] * (len(operands) - 1), anywhere],
+            in_specs=[*[in_vmem] * len(operands), anywhere],
             out_specs=[in_vmem] * len(outs),
             compiler_params=pltpu.CompilerParams(vmem_limit_bytes=16 << 20),
         )(*operands, after[-1])
@@ -361,36 +381,38 @@
         return lax.ppermute(value, ("expert", "section"), perm)
 
     halves = (0, 1)
-    straight, first, second, third = [None] * 2, [None] * 2, [None] * 2, [None] * 2
-    done, was, here, back, last = [None] * 2, [None] * 2, [None] * 2, [None] * 2, [None] * 2
+    inputs = [own_rows, other_rows, arriving_microgroups]
+    both, *sent = stage(tick_0, None, inputs, (2 * num_rows, size, size))
+    first = [ahead(sent[h], 2, True) for h in halves]
+    straight = ahead(both, 0, True)
+    done, second = [None] * 2, [None] * 2
     for h in halves:
-        both, sent = stage(tick_0, h, [own_rows, other_rows, arriving_microgroups], (2 * size, size))
-        first[h] = ahead(sent, 2, True)
-        straight[h] = ahead(both, 0, True)
-    for h in halves:
-        inputs = [straight[h], first[h], arriving_microgroups]
+        inputs = [straight, first[h], arriving_microgroups]
         done[h], sent = stage(tick_1_before, h, inputs, (size, size))
         second[h] = swapped(sent, "expert", 1)
+    after_1, here = [None] * 2, [None] * 2
     for h in halves:
-        inputs = [straight[h], first[h], second[h], done[h], arriving_microgroups]
-        both, was[h], here[h] = stage(tick_1_after, h, inputs, (2 * size, size, size))
-        straight[h] = ahead(both, 0, False)
-        was[h] = turned(was[h], "section", 1)
+        inputs = [straight, done[h], arriving_microgroups, *first[: h + 1], *second[: h + 1]]
+        outs = (2 * size, size, num_rows)[: h + 2]
+        both, here[h], *was = stage(tick_1_after, h, inputs, outs)
+        after_1[h] = ahead(both, 0, False)
+    was = turned(was[0], "section", 1)
+    third, back, last = [None] * 2, [None] * 2, [None] * 2
     for h in halves:
-        (sent,) = stage(tick_2_before, h, [straight[h], fresh_other], (size,))
+        (sent,) = stage(tick_2_before, h, [after_1[h], fresh_other], (size,))
         third[h] = swapped(sent, "expert", 1)
     for h in halves:
         back[h] = turned(third[h], "section", 1)
-        (last[h],) = stage(tick_2_after, h, [straight[h], third[h], arriving_microgroups], (size,))
-    operands = [part for h in halves for part in (was[h], here[h], back[h], last[h])]
+        (last[h],) = stage(tick_2_after, h, [after_1[h], third[h], arriving_microgroups], (size,))
+    operands = [table, was, *[part for h in halves for part in (here[h], back[h], last[h])]]
     return pl.pallas_call(
         gather_kernel,
         out_shape=jax.ShapeDtypeStruct((1, TICKS, num_rows, width), jnp.bfloat16),
-        in_specs=[in_smem, *[in_vmem] * len(operands)],
+        in_specs=[in_vmem] * len(operands),
         out_specs=in_vmem,
         compiler_params=limited,
         name="gather",
-    )(table, *operands)
+    )(*operands)
 
 
 def solution(mesh):

time: 102 us -> 96.5 us (0.946)
  Pallas kernels: 24 us -> 17.3 us
  starting transfers between devices: 45.6 us -> 52 us
  waiting for transfers between devices: 30.1 us -> 26.2 us
  local copies, waits for them, and re-layouts: 1.53 us -> 0.04 us
    pallas_call x11 -> x10, Pallas kernels: 18.4 us -> 12.3 us  [the longest x9 11.6 us: stage(): pl.pallas_call(body if half is None else functools.partial(body, half), o...]
    ppermute x7 -> x6, starting transfers between devices: 6.36 us -> 11.4 us  [turned(): lax.ppermute(value, axis, [((i + steps) % count, i) for i in range(count)])]
    ppermute x6 -> x5, waiting for transfers between devices: 7.6 us -> 4.98 us  [ahead(): return lax.ppermute(value, ('expert', 'section'), perm)]
    ppermute x1, starting transfers between devices: 2.21 us -> 4.81 us  [pairs_per_device(): lax.ppermute(arriving_microgroups[1], ('expert', 'section'), pairs)]
    ppermute x18, waiting for transfers between devices: 19.1 us -> 17.1 us  [swapped(): lax.ppermute(x, axis, [(i, i ^ 1 << bit) for i in range(lax.axis_size(axi...]
    ppermute x6 -> x5, starting transfers between devices: 10 us -> 8.42 us  [ahead(): return lax.ppermute(value, ('expert', 'section'), perm)]
    unnamed x18 -> x14, local copies, waits for them, and re-layouts: 1.52 us -> 0.03 us
    ppermute x7 -> x6, waiting for transfers between devices: 3.4 us -> 3.4 us  [turned(): lax.ppermute(value, axis, [((i + steps) % count, i) for i in range(count)])]
  transfers between devices with their start and end apart: 32 -> 30, of which waited for: 15 -> 13; matrix products, arithmetic and copies ran while one was open for 0% -> 0% of each run, Pallas kernels for 17% -> 11%
where the time goes in v2:
time: 96.5 us; the launch traced here: 95.9 us
  starting transfers between devices  52 us (54%)
  waiting for transfers between devices  26.2 us (27%)
  Pallas kernels  17.3 us (18%)
    ppermute x18, starting transfers between devices, swapped(): lax.ppermute(x, axis, [(i, i ^ 1 << bit) for i in range(lax.axis_size(axi...  27.4 us
    ppermute x18, waiting for transfers between devices, swapped(): lax.ppermute(x, axis, [(i, i ^ 1 << bit) for i in range(lax.axis_size(axi...  17.1 us
    pallas_call x9, Pallas kernels, stage(): pl.pallas_call(body if half is None else functools.partial(body, half), o...  11.6 us
    ppermute x6, starting transfers between devices, turned(): lax.ppermute(value, axis, [((i + steps) % count, i) for i in range(count)])  11.4 us
    ppermute x5, starting transfers between devices, ahead(): return lax.ppermute(value, ('expert', 'section'), perm)  8.42 us
    ppermute x5, waiting for transfers between devices, ahead(): return lax.ppermute(value, ('expert', 'section'), perm)  4.98 us
    ppermute x1, starting transfers between devices, pairs_per_device(): lax.ppermute(arriving_microgroups[1], ('expert', 'section'), pairs)  4.81 us
    pallas_call x2, Pallas kernels, cut(): pl.pallas_call(functools.partial(cut_kernel, some), out_shape=[jax.ShapeD...  3.98 us
  transfers between devices with their start and end apart: 30, of which 13 were waited for; matrix products, arithmetic and copies ran while one was open for 0% of the time, Pallas kernels for 11%

profile of v2, /device:TPU:0, one launch (start us, length us, event | category | flops | bytes accessed | tf_op | source)
XLA Modules:
  0.0 95.9 jit_solution(112786078918143425)
XLA Ops:
  0.0 2.4 %shard_map.74 = (bf16[128,768]{1,0:T(8,128)(2,1)}, bf16[128,768]{1,0:T(8,128)(2,1)}, bf16[112,768]{1,0:T(8,128)(2,1)}, bf16[112,768]{1,0:T(8,128)(2,1)}, bf16[11...) custom-call(bf16[768,768]{1,0:T(8,128)(2,1)} %bitcast.8, bf16[768,768]{1,0:T(8,128)(2,1)} %bitcast.20), custom_call_target="tpu_custom_call" | custom-call | tf_op jit(solution)/shard_map/pallas_call | solution.py:315
  2.4 3.1 %collective-permute-start.10 = (bf16[112,768]{1,0:T(8,128)(2,1)}, bf16[112,768]{1,0:T(8,128)(2,1)S(1)}, u32[]{:S(2)}, u32[]{:S(2)}) collective-permute-start(bf16[112,768]{1,0:T(8,128)(2,1)} %get-tuple-element.25), channel_id=1, source_target_pairs={{0,4},{4,0},{8,12},{12,8},{1,5},{5,1},{9,13},{13,9},{2,6},{6,2},{1... | collective-permute-start | bytes 516104 | tf_op jit(solution)/shard_map/ppermute | solution.py:15
  5.6 1.9 %collective-permute-start.12 = (bf16[112,768]{1,0:T(8,128)(2,1)}, bf16[112,768]{1,0:T(8,128)(2,1)S(1)}, u32[]{:S(2)}, u32[]{:S(2)}) collective-permute-start(bf16[112,768]{1,0:T(8,128)(2,1)} %get-tuple-element.26), channel_id=1, source_target_pairs={{0,4},{4,0},{8,12},{12,8},{1,5},{5,1},{9,13},{13,9},{2,6},{6,2},{1... | collective-permute-start | bytes 516104 | tf_op jit(solution)/shard_map/ppermute | solution.py:15
  10.9 1.9 %collective-permute-done.1.second_ref = s32[3,1,128]{2,1,0:T(1,128)S(1)} collective-permute-done((s32[3,1,128]{2,1,0:T(1,128)S(1)}, s32[3,1,128]{2,1,0:T(1,128)S(1)}, u32[]{:S(2)}, u32[]{:S(2)}) %collective-permute-start.1) | collective-permute-done | bytes 1568 | tf_op jit(solution)/shard_map/ppermute | solution.py:312
  17.8 1.8 %collective-permute-start.4 = (bf16[128,768]{1,0:T(8,128)(2,1)}, bf16[128,768]{1,0:T(8,128)(2,1)S(1)}, u32[]{:S(2)}, u32[]{:S(2)}) collective-permute-start(bf16[128,768]{1,0:T(8,128)(2,1)} %shard_map.73), channel_id=1, source_target_pairs={{0,4},{4,0},{8,12},{12,8},{1,5},{5,1},{9,13},{13,9},{2,6},{6,2},{1... | collective-permute-start | bytes 589832 | tf_op jit(solution)/shard_map/ppermute | solution.py:15
  21.5 2.0 %collective-permute-start.13 = (bf16[112,768]{1,0:T(8,128)(2,1)S(1)}, bf16[112,768]{1,0:T(8,128)(2,1)S(1)}, u32[]{:S(2)}, u32[]{:S(2)}) collective-permute-start(bf16[112,768]{1,0:T(8,128)(2,1)S(1)} %collective-permute-done.12.refs_2_), channel_id=1, source_target_pairs={{0,16},{16,0},{1,17},{17,1},{2,18},{18,2},{3,19},{19,3},{4,20},{20... | collective-permute-start | bytes 516104 | tf_op jit(solution)/shard_map/ppermute | solution.py:15
  23.4 2.2 %collective-permute-done.6.refs_2_ = bf16[128,768]{1,0:T(8,128)(2,1)S(1)} collective-permute-done((bf16[128,768]{1,0:T(8,128)(2,1)}, bf16[128,768]{1,0:T(8,128)(2,1)S(1)}, u32[]{:S(2)}, u32[]{:S(2)}) %collective-permute-start.6) | collective-permute-done | bytes 196640 | tf_op jit(solution)/shard_map/ppermute | solution.py:15
  25.7 2.0 %collective-permute-start.7 = (bf16[128,768]{1,0:T(8,128)(2,1)S(1)}, bf16[128,768]{1,0:T(8,128)(2,1)S(1)}, u32[]{:S(2)}, u32[]{:S(2)}) collective-permute-start(bf16[128,768]{1,0:T(8,128)(2,1)S(1)} %collective-permute-done.6.refs_2_), channel_id=1, source_target_pairs={{0,16},{16,0},{1,17},{17,1},{2,18},{18,2},{3,19},{19,3},{4,20},{20... | collective-permute-start | bytes 589832 | tf_op jit(solution)/shard_map/ppermute | solution.py:15
  27.6 2.2 %collective-permute-done.8.refs_4_ = bf16[128,768]{1,0:T(8,128)(2,1)S(1)} collective-permute-done((bf16[128,768]{1,0:T(8,128)(2,1)}, bf16[128,768]{1,0:T(8,128)(2,1)S(1)}, u32[]{:S(2)}, u32[]{:S(2)}) %collective-permute-start.8) | collective-permute-done | bytes 196640 | tf_op jit(solution)/shard_map/ppermute | solution.py:15
  29.9 2.0 %collective-permute-start.9 = (bf16[128,768]{1,0:T(8,128)(2,1)S(1)}, bf16[128,768]{1,0:T(8,128)(2,1)S(1)}, u32[]{:S(2)}, u32[]{:S(2)}) collective-permute-start(bf16[128,768]{1,0:T(8,128)(2,1)S(1)} %collective-permute-done.8.refs_4_), channel_id=1, source_target_pairs={{0,16},{16,0},{1,17},{17,1},{2,18},{18,2},{3,19},{19,3},{4,20},{20... | collective-permute-start | bytes 589832 | tf_op jit(solution)/shard_map/ppermute | solution.py:15
  35.0 2.6 %collective-permute-start.3 = (bf16[128,768]{1,0:T(8,128)(2,1)S(1)}, bf16[128,768]{1,0:T(8,128)(2,1)S(1)}, u32[]{:S(2)}, u32[]{:S(2)}) collective-permute-start(bf16[128,768]{1,0:T(8,128)(2,1)S(1)} %bitcast.32), channel_id=1, source_target_pairs={{0,8},{4,12},{8,0},{12,4},{1,9},{5,13},{9,1},{13,5},{2,10},{6,14},... | collective-permute-start | bytes 589832 | tf_op jit(solution)/shard_map/ppermute | solution.py:15
  38.7 6.6 %collective-permute-done.15.refs_5_ = bf16[112,768]{1,0:T(8,128)(2,1)S(1)} collective-permute-done((bf16[112,768]{1,0:T(8,128)(2,1)S(1)}, bf16[112,768]{1,0:T(8,128)(2,1)S(1)}, u32[]{:S(2)}, u32[]{:S(2)}) %collective-permute-start.15) | collective-permute-done | bytes 172064 | tf_op jit(solution)/shard_map/ppermute | solution.py:15
  45.6 1.9 %shard_map.77 = (bf16[256,768]{1,0:T(8,128)(2,1)S(1)}, bf16[64,768]{1,0:T(8,128)(2,1)S(1)}, bf16[64,768]{1,0:T(8,128)(2,1)S(1)}) custom-call(s32[8,128]{1,0:T(8,128)S(1)} %table.1.table_ref, bf16[128,768]{1,0:T(8,128)(2,1)S(1)} %bitcast.33, bf16[128,768]{1,0:T(8,128)(2,1)S(1)} %collective-permute-done.3.partner_ref, bf16[2,128,768]{2,1,0:T(8,128)(2,1)S(1)} %copy-done.2, ...), custom_call_target="tpu_custom_call" | custom-call | tf_op jit(solution)/shard_map/pallas_call | solution.py:364
  47.6 2.8 %collective-permute-start.19 = (bf16[64,768]{1,0:T(8,128)(2,1)S(1)}, bf16[64,768]{1,0:T(8,128)(2,1)S(1)}, u32[]{:S(2)}, u32[]{:S(2)}) collective-permute-start(bf16[64,768]{1,0:T(8,128)(2,1)S(1)} %get-tuple-element.31), channel_id=1, source_target_pairs={{0,9},{1,10},{2,11},{3,8},{4,13},{5,14},{6,15},{7,12},{8,1},{9,2},... | collective-permute-start | bytes 294920 | tf_op jit(solution)/shard_map/ppermute | solution.py:381
  51.2 5.0 %collective-permute-done.19.first_ref.refs_0_ = bf16[64,768]{1,0:T(8,128)(2,1)S(1)} collective-permute-done((bf16[64,768]{1,0:T(8,128)(2,1)S(1)}, bf16[64,768]{1,0:T(8,128)(2,1)S(1)}, u32[]{:S(2)}, u32[]{:S(2)}) %collective-permute-start.19) | collective-permute-done | bytes 98336 | tf_op jit(solution)/shard_map/ppermute | solution.py:381
  57.4 3.4 %collective-permute-start.20 = (bf16[64,768]{1,0:T(8,128)(2,1)S(1)}, bf16[64,768]{1,0:T(8,128)(2,1)S(1)}, u32[]{:S(2)}, u32[]{:S(2)}) collective-permute-start(bf16[64,768]{1,0:T(8,128)(2,1)S(1)} %get-tuple-element.34), channel_id=1, source_target_pairs={{0,8},{4,12},{8,0},{12,4},{1,9},{5,13},{9,1},{13,5},{2,10},{6,14},... | collective-permute-start | bytes 294920 | tf_op jit(solution)/shard_map/ppermute | solution.py:15
  62.1 4.8 %collective-permute-start.24 = (bf16[128,768]{1,0:T(8,128)(2,1)S(1)}, bf16[128,768]{1,0:T(8,128)(2,1)S(1)}, u32[]{:S(2)}, u32[]{:S(2)}) collective-permute-start(bf16[128,768]{1,0:T(8,128)(2,1)S(1)} %slice_bitcast_fusion), channel_id=1, source_target_pairs={{0,8},{4,12},{8,0},{12,4},{16,24},{20,28},{24,16},{28,20}} | collective-permute-start | bytes 589832 | tf_op jit(solution)/shard_map/ppermute | solution.py:358
  68.2 2.2 %collective-permute-start.23 = (bf16[128,768]{1,0:T(8,128)(2,1)S(1)}, bf16[128,768]{1,0:T(8,128)(2,1)S(1)}, u32[]{:S(2)}, u32[]{:S(2)}) collective-permute-start(bf16[128,768]{1,0:T(8,128)(2,1)S(1)} %get-tuple-element.36.refs_10_), channel_id=1, source_target_pairs={{0,1},{1,2},{2,3},{4,5},{5,6},{6,7},{8,9},{9,10},{10,11},{12,13},{... | collective-permute-start | bytes 589832 | tf_op jit(solution)/shard_map/ppermute | solution.py:381
  72.0 2.6 %collective-permute-start.27 = (bf16[128,768]{1,0:T(8,128)(2,1)S(1)}, bf16[128,768]{1,0:T(8,128)(2,1)S(1)}, u32[]{:S(2)}, u32[]{:S(2)}) collective-permute-start(bf16[128,768]{1,0:T(8,128)(2,1)S(1)} %get-tuple-element.39.refs_6_), channel_id=1, source_target_pairs={{0,1},{1,2},{2,3},{4,5},{5,6},{6,7},{8,9},{9,10},{10,11},{12,13},{... | collective-permute-start | bytes 589832 | tf_op jit(solution)/shard_map/ppermute | solution.py:381
  77.7 2.1 %collective-permute-start.22 = (bf16[128,768]{1,0:T(8,128)(2,1)S(1)}, bf16[128,768]{1,0:T(8,128)(2,1)S(1)}, u32[]{:S(2)}, u32[]{:S(2)}) collective-permute-start(bf16[128,768]{1,0:T(8,128)(2,1)S(1)} %get-tuple-element.37), channel_id=1, source_target_pairs={{1,0},{2,1},{3,2},{0,3},{5,4},{6,5},{7,6},{4,7},{9,8},{10,9},{11,1... | collective-permute-start | bytes 589832 | tf_op jit(solution)/shard_map/ppermute | solution.py:312
  79.8 2.6 %collective-permute-start.25 = (bf16[64,768]{1,0:T(8,128)(2,1)S(1)}, bf16[64,768]{1,0:T(8,128)(2,1)S(1)}, u32[]{:S(2)}, u32[]{:S(2)}) collective-permute-start(bf16[64,768]{1,0:T(8,128)(2,1)S(1)} %shard_map.82.refs_6_), channel_id=1, source_target_pairs={{0,8},{4,12},{8,0},{12,4},{1,9},{5,13},{9,1},{13,5},{2,10},{6,14},... | collective-permute-start | bytes 294920 | tf_op jit(solution)/shard_map/ppermute | solution.py:15
  83.2 3.4 %collective-permute-start.29 = (bf16[64,768]{1,0:T(8,128)(2,1)S(1)}, bf16[64,768]{1,0:T(8,128)(2,1)S(1)}, u32[]{:S(2)}, u32[]{:S(2)}) collective-permute-start(bf16[64,768]{1,0:T(8,128)(2,1)S(1)} %collective-permute-done.28.third_ref), channel_id=1, source_target_pairs={{1,0},{2,1},{3,2},{0,3},{5,4},{6,5},{7,6},{4,7},{9,8},{10,9},{11,1... | collective-permute-start | bytes 294920 | tf_op jit(solution)/shard_map/ppermute | solution.py:312
  86.6 3.1 %collective-permute-done.25.third_ref = bf16[64,768]{1,0:T(8,128)(2,1)S(1)} collective-permute-done((bf16[64,768]{1,0:T(8,128)(2,1)S(1)}, bf16[64,768]{1,0:T(8,128)(2,1)S(1)}, u32[]{:S(2)}, u32[]{:S(2)}) %collective-permute-start.25) | collective-permute-done | bytes 98336 | tf_op jit(solution)/shard_map/ppermute | solution.py:15
  89.6 2.9 %collective-permute-start.26 = (bf16[64,768]{1,0:T(8,128)(2,1)S(1)}, bf16[64,768]{1,0:T(8,128)(2,1)S(1)}, u32[]{:S(2)}, u32[]{:S(2)}) collective-permute-start(bf16[64,768]{1,0:T(8,128)(2,1)S(1)} %collective-permute-done.25.third_ref), channel_id=1, source_target_pairs={{1,0},{2,1},{3,2},{0,3},{5,4},{6,5},{7,6},{4,7},{9,8},{10,9},{11,1... | collective-permute-start | bytes 294920 | tf_op jit(solution)/shard_map/ppermute | solution.py:312
  (66 shorter events, 28.3 us)
Async XLA Ops:
  2.4 15.4 %collective-permute-start.10 = (bf16[112,768]{1,0:T(8,128)(2,1)}, bf16[112,768]{1,0:T(8,128)(2,1)S(1)}, u32[]{:S(2)}, u32[]{:S(2)}) collective-permute-start(bf16[112,768]{1,0:T(8,128)(2,1)} %get-tuple-element.25), channel_id=1, source_target_pairs={{0,4},{4,0},{8,12},{12,8},{1,5},{5,1},{9,13},{13,9},{2,6},{6,2},{1... | collective-permute-start | bytes 516104 | tf_op jit(solution)/shard_map/ppermute | solution.py:15
  5.5 12.0 %collective-permute-start.16 = (bf16[96,768]{1,0:T(8,128)(2,1)}, bf16[96,768]{1,0:T(8,128)(2,1)S(1)}, u32[]{:S(2)}, u32[]{:S(2)}) collective-permute-start(bf16[96,768]{1,0:T(8,128)(2,1)} %get-tuple-element.28), channel_id=1, source_target_pairs={{0,4},{4,0},{8,12},{12,8},{1,5},{5,1},{9,13},{13,9},{2,6},{6,2},{1... | collective-permute-start | bytes 442376 | tf_op jit(solution)/shard_map/ppermute | solution.py:15
  5.6 14.0 %collective-permute-start.12 = (bf16[112,768]{1,0:T(8,128)(2,1)}, bf16[112,768]{1,0:T(8,128)(2,1)S(1)}, u32[]{:S(2)}, u32[]{:S(2)}) collective-permute-start(bf16[112,768]{1,0:T(8,128)(2,1)} %get-tuple-element.26), channel_id=1, source_target_pairs={{0,4},{4,0},{8,12},{12,8},{1,5},{5,1},{9,13},{13,9},{2,6},{6,2},{1... | collective-permute-start | bytes 516104 | tf_op jit(solution)/shard_map/ppermute | solution.py:15
  7.6 13.9 %collective-permute-start.14 = (bf16[112,768]{1,0:T(8,128)(2,1)}, bf16[112,768]{1,0:T(8,128)(2,1)S(1)}, u32[]{:S(2)}, u32[]{:S(2)}) collective-permute-start(bf16[112,768]{1,0:T(8,128)(2,1)} %get-tuple-element.27), channel_id=1, source_target_pairs={{0,4},{4,0},{8,12},{12,8},{1,5},{5,1},{9,13},{13,9},{2,6},{6,2},{1... | collective-permute-start | bytes 516104 | tf_op jit(solution)/shard_map/ppermute | solution.py:15
  15.8 9.9 %collective-permute-start.6 = (bf16[128,768]{1,0:T(8,128)(2,1)}, bf16[128,768]{1,0:T(8,128)(2,1)S(1)}, u32[]{:S(2)}, u32[]{:S(2)}) collective-permute-start(bf16[128,768]{1,0:T(8,128)(2,1)} %get-tuple-element.23), channel_id=1, source_target_pairs={{0,4},{4,0},{8,12},{12,8},{1,5},{5,1},{9,13},{13,9},{2,6},{6,2},{1... | collective-permute-start | bytes 589832 | tf_op jit(solution)/shard_map/ppermute | solution.py:15
  17.5 12.4 %collective-permute-start.8 = (bf16[128,768]{1,0:T(8,128)(2,1)}, bf16[128,768]{1,0:T(8,128)(2,1)S(1)}, u32[]{:S(2)}, u32[]{:S(2)}) collective-permute-start(bf16[128,768]{1,0:T(8,128)(2,1)} %get-tuple-element.24), channel_id=1, source_target_pairs={{0,4},{4,0},{8,12},{12,8},{1,5},{5,1},{9,13},{13,9},{2,6},{6,2},{1... | collective-permute-start | bytes 589832 | tf_op jit(solution)/shard_map/ppermute | solution.py:15
  17.8 15.5 %collective-permute-start.4 = (bf16[128,768]{1,0:T(8,128)(2,1)}, bf16[128,768]{1,0:T(8,128)(2,1)S(1)}, u32[]{:S(2)}, u32[]{:S(2)}) collective-permute-start(bf16[128,768]{1,0:T(8,128)(2,1)} %shard_map.73), channel_id=1, source_target_pairs={{0,4},{4,0},{8,12},{12,8},{1,5},{5,1},{9,13},{13,9},{2,6},{6,2},{1... | collective-permute-start | bytes 589832 | tf_op jit(solution)/shard_map/ppermute | solution.py:15
  19.6 15.4 %collective-permute-start.11 = (bf16[112,768]{1,0:T(8,128)(2,1)S(1)}, bf16[112,768]{1,0:T(8,128)(2,1)S(1)}, u32[]{:S(2)}, u32[]{:S(2)}) collective-permute-start(bf16[112,768]{1,0:T(8,128)(2,1)S(1)} %collective-permute-done.10.refs_0_), channel_id=1, source_target_pairs={{0,16},{16,0},{1,17},{17,1},{2,18},{18,2},{3,19},{19,3},{4,20},{20... | collective-permute-start | bytes 516104 | tf_op jit(solution)/shard_map/ppermute | solution.py:15
  21.5 16.1 %collective-permute-start.13 = (bf16[112,768]{1,0:T(8,128)(2,1)S(1)}, bf16[112,768]{1,0:T(8,128)(2,1)S(1)}, u32[]{:S(2)}, u32[]{:S(2)}) collective-permute-start(bf16[112,768]{1,0:T(8,128)(2,1)S(1)} %collective-permute-done.12.refs_2_), channel_id=1, source_target_pairs={{0,16},{16,0},{1,17},{17,1},{2,18},{18,2},{3,19},{19,3},{4,20},{20... | collective-permute-start | bytes 516104 | tf_op jit(solution)/shard_map/ppermute | solution.py:15
  25.7 19.7 %collective-permute-start.7 = (bf16[128,768]{1,0:T(8,128)(2,1)S(1)}, bf16[128,768]{1,0:T(8,128)(2,1)S(1)}, u32[]{:S(2)}, u32[]{:S(2)}) collective-permute-start(bf16[128,768]{1,0:T(8,128)(2,1)S(1)} %collective-permute-done.6.refs_2_), channel_id=1, source_target_pairs={{0,16},{16,0},{1,17},{17,1},{2,18},{18,2},{3,19},{19,3},{4,20},{20... | collective-permute-start | bytes 589832 | tf_op jit(solution)/shard_map/ppermute | solution.py:15
  29.9 15.5 %collective-permute-start.9 = (bf16[128,768]{1,0:T(8,128)(2,1)S(1)}, bf16[128,768]{1,0:T(8,128)(2,1)S(1)}, u32[]{:S(2)}, u32[]{:S(2)}) collective-permute-start(bf16[128,768]{1,0:T(8,128)(2,1)S(1)} %collective-permute-done.8.refs_4_), channel_id=1, source_target_pairs={{0,16},{16,0},{1,17},{17,1},{2,18},{18,2},{3,19},{19,3},{4,20},{20... | collective-permute-start | bytes 589832 | tf_op jit(solution)/shard_map/ppermute | solution.py:15
  33.3 12.2 %collective-permute-start.5 = (bf16[128,768]{1,0:T(8,128)(2,1)S(1)}, bf16[128,768]{1,0:T(8,128)(2,1)S(1)}, u32[]{:S(2)}, u32[]{:S(2)}) collective-permute-start(bf16[128,768]{1,0:T(8,128)(2,1)S(1)} %collective-permute-done.4.refs_0_), channel_id=1, source_target_pairs={{0,16},{16,0},{1,17},{17,1},{2,18},{18,2},{3,19},{19,3},{4,20},{20... | collective-permute-start | bytes 589832 | tf_op jit(solution)/shard_map/ppermute | solution.py:15
  35.0 10.6 %collective-permute-start.3 = (bf16[128,768]{1,0:T(8,128)(2,1)S(1)}, bf16[128,768]{1,0:T(8,128)(2,1)S(1)}, u32[]{:S(2)}, u32[]{:S(2)}) collective-permute-start(bf16[128,768]{1,0:T(8,128)(2,1)S(1)} %bitcast.32), channel_id=1, source_target_pairs={{0,8},{4,12},{8,0},{12,4},{1,9},{5,13},{9,1},{13,5},{2,10},{6,14},... | collective-permute-start | bytes 589832 | tf_op jit(solution)/shard_map/ppermute | solution.py:15
  37.5 7.8 %collective-permute-start.15 = (bf16[112,768]{1,0:T(8,128)(2,1)S(1)}, bf16[112,768]{1,0:T(8,128)(2,1)S(1)}, u32[]{:S(2)}, u32[]{:S(2)}) collective-permute-start(bf16[112,768]{1,0:T(8,128)(2,1)S(1)} %collective-permute-done.14.refs_4_), channel_id=1, source_target_pairs={{0,16},{16,0},{1,17},{17,1},{2,18},{18,2},{3,19},{19,3},{4,20},{20... | collective-permute-start | bytes 516104 | tf_op jit(solution)/shard_map/ppermute | solution.py:15
  47.5 8.7 %collective-permute-start.17 = (bf16[256,768]{1,0:T(8,128)(2,1)S(1)}, bf16[256,768]{1,0:T(8,128)(2,1)S(1)}, u32[]{:S(2)}, u32[]{:S(2)}) collective-permute-start(bf16[256,768]{1,0:T(8,128)(2,1)S(1)} %get-tuple-element.29.refs_6_), channel_id=1, source_target_pairs={{0,1},{1,2},{2,3},{3,0},{4,5},{5,6},{6,7},{7,4},{8,9},{9,10},{10,1... | collective-permute-start | bytes 1179656 | tf_op jit(solution)/shard_map/ppermute | solution.py:381
  47.6 8.6 %collective-permute-start.19 = (bf16[64,768]{1,0:T(8,128)(2,1)S(1)}, bf16[64,768]{1,0:T(8,128)(2,1)S(1)}, u32[]{:S(2)}, u32[]{:S(2)}) collective-permute-start(bf16[64,768]{1,0:T(8,128)(2,1)S(1)} %get-tuple-element.31), channel_id=1, source_target_pairs={{0,9},{1,10},{2,11},{3,8},{4,13},{5,14},{6,15},{7,12},{8,1},{9,2},... | collective-permute-start | bytes 294920 | tf_op jit(solution)/shard_map/ppermute | solution.py:381
  50.4 10.4 %collective-permute-start.18 = (bf16[64,768]{1,0:T(8,128)(2,1)S(1)}, bf16[64,768]{1,0:T(8,128)(2,1)S(1)}, u32[]{:S(2)}, u32[]{:S(2)}) collective-permute-start(bf16[64,768]{1,0:T(8,128)(2,1)S(1)} %get-tuple-element.30), channel_id=1, source_target_pairs={{0,9},{1,10},{2,11},{3,8},{4,13},{5,14},{6,15},{7,12},{8,1},{9,2},... | collective-permute-start | bytes 294920 | tf_op jit(solution)/shard_map/ppermute | solution.py:381
  57.4 9.5 %collective-permute-start.20 = (bf16[64,768]{1,0:T(8,128)(2,1)S(1)}, bf16[64,768]{1,0:T(8,128)(2,1)S(1)}, u32[]{:S(2)}, u32[]{:S(2)}) collective-permute-start(bf16[64,768]{1,0:T(8,128)(2,1)S(1)} %get-tuple-element.34), channel_id=1, source_target_pairs={{0,8},{4,12},{8,0},{12,4},{1,9},{5,13},{9,1},{13,5},{2,10},{6,14},... | collective-permute-start | bytes 294920 | tf_op jit(solution)/shard_map/ppermute | solution.py:15
  62.0 8.7 %collective-permute-start.21 = (bf16[64,768]{1,0:T(8,128)(2,1)S(1)}, bf16[64,768]{1,0:T(8,128)(2,1)S(1)}, u32[]{:S(2)}, u32[]{:S(2)}) collective-permute-start(bf16[64,768]{1,0:T(8,128)(2,1)S(1)} %get-tuple-element.35), channel_id=1, source_target_pairs={{0,8},{4,12},{8,0},{12,4},{1,9},{5,13},{9,1},{13,5},{2,10},{6,14},... | collective-permute-start | bytes 294920 | tf_op jit(solution)/shard_map/ppermute | solution.py:15
  62.1 13.1 %collective-permute-start.24 = (bf16[128,768]{1,0:T(8,128)(2,1)S(1)}, bf16[128,768]{1,0:T(8,128)(2,1)S(1)}, u32[]{:S(2)}, u32[]{:S(2)}) collective-permute-start(bf16[128,768]{1,0:T(8,128)(2,1)S(1)} %slice_bitcast_fusion), channel_id=1, source_target_pairs={{0,8},{4,12},{8,0},{12,4},{16,24},{20,28},{24,16},{28,20}} | collective-permute-start | bytes 589832 | tf_op jit(solution)/shard_map/ppermute | solution.py:358
  68.2 7.1 %collective-permute-start.23 = (bf16[128,768]{1,0:T(8,128)(2,1)S(1)}, bf16[128,768]{1,0:T(8,128)(2,1)S(1)}, u32[]{:S(2)}, u32[]{:S(2)}) collective-permute-start(bf16[128,768]{1,0:T(8,128)(2,1)S(1)} %get-tuple-element.36.refs_10_), channel_id=1, source_target_pairs={{0,1},{1,2},{2,3},{4,5},{5,6},{6,7},{8,9},{9,10},{10,11},{12,13},{... | collective-permute-start | bytes 589832 | tf_op jit(solution)/shard_map/ppermute | solution.py:381
  77.7 17.3 %collective-permute-start.22 = (bf16[128,768]{1,0:T(8,128)(2,1)S(1)}, bf16[128,768]{1,0:T(8,128)(2,1)S(1)}, u32[]{:S(2)}, u32[]{:S(2)}) collective-permute-start(bf16[128,768]{1,0:T(8,128)(2,1)S(1)} %get-tuple-element.37), channel_id=1, source_target_pairs={{1,0},{2,1},{3,2},{0,3},{5,4},{6,5},{7,6},{4,7},{9,8},{10,9},{11,1... | collective-permute-start | bytes 589832 | tf_op jit(solution)/shard_map/ppermute | solution.py:312
  79.8 9.8 %collective-permute-start.25 = (bf16[64,768]{1,0:T(8,128)(2,1)S(1)}, bf16[64,768]{1,0:T(8,128)(2,1)S(1)}, u32[]{:S(2)}, u32[]{:S(2)}) collective-permute-start(bf16[64,768]{1,0:T(8,128)(2,1)S(1)} %shard_map.82.refs_6_), channel_id=1, source_target_pairs={{0,8},{4,12},{8,0},{12,4},{1,9},{5,13},{9,1},{13,5},{2,10},{6,14},... | collective-permute-start | bytes 294920 | tf_op jit(solution)/shard_map/ppermute | solution.py:15
  83.2 11.8 %collective-permute-start.29 = (bf16[64,768]{1,0:T(8,128)(2,1)S(1)}, bf16[64,768]{1,0:T(8,128)(2,1)S(1)}, u32[]{:S(2)}, u32[]{:S(2)}) collective-permute-start(bf16[64,768]{1,0:T(8,128)(2,1)S(1)} %collective-permute-done.28.third_ref), channel_id=1, source_target_pairs={{1,0},{2,1},{3,2},{0,3},{5,4},{6,5},{7,6},{4,7},{9,8},{10,9},{11,1... | collective-permute-start | bytes 294920 | tf_op jit(solution)/shard_map/ppermute | solution.py:312
  (13 other events, 218.7 us)
